TPU v7x, 256 devices: a whole 4x4x8 slice. The times are simulated.
256 devices in a mesh: shell: 8 (over z), sector: 32 (over x, y, core).
Axes of the slice: x: 4, y: 4, z: 8, core: 2. Of those that a mesh axis runs over, the one named last changes fastest.
Arguments:
- bricks: bfloat16 [8, 256, 32, 512], P('shell', 'sector'), may hold values from -6 to 6
- conv_w: bfloat16 [32, 864], replicated, may hold values from -0.21875 to 0.21875
- conv_b: float32 [32], replicated, may hold values from -3 to 3
- head_w1: bfloat16 [32, 64], replicated, may hold values from -1 to 1
- head_b1: float32 [64], replicated, may hold values from -3 to 3
- head_w2: float32 [64, 2], replicated, may hold values from -0.75 to 0.75
- queries: int32 [8, 1024, 256], P('shell', 'sector'), may hold values from -1 to 4095, as said below
- sample_src: int32 [8, 131072], P('shell', 'sector'), may hold values from 0 to 8191, as said below
- depth_target: float32 [16384], P('sector'), may hold values from 0.1 to 0.9
- inten_target: float32 [16384], P('sector'), may hold values from 0 to 1
- drop_label: int32 [16384], P('sector'), may hold values 0 or 1
Outputs:
- loss_mean: float32 [], replicated
- grad_conv_w: float32 [32, 864], replicated
- grad_conv_b: float32 [32], replicated
- grad_head_w1: float32 [32, 64], replicated
- grad_head_b1: float32 [64], replicated
- grad_head_w2: float32 [64, 2], replicated
- grad_bricks: bfloat16 [8, 256, 32, 512], P('shell', 'sector')
- ray_depth: float32 [16384], P('sector')
Inputs may be any that keep to these rules, and one draw needn't show every extreme that they name: `queries`: entry of the buffer from a device of sector v to owner w: a cell address (brick of the owner times 512 plus cell) or -1 for an empty slot. Every sample of a device holds exactly one live slot, named by sample_src as w * 256 + slot. In every shell one owner receives full buffers of 256 from every sector. `sample_src`: A slot w * 256 + slot of the sample's own device; distinct samples of a device have distinct slots.
All inputs are finite; a program needn't handle non-finite values. No bound on the sum of `drop_label` on one device may be relied on, other than what follows from the above.
Results may differ from a plain program's by a relative error of at most 0.0015.
The roundings to bfloat16 on the way count: a program that leaves them out, or rounds other values in their place, can miss the bound.
Values may be sent and summed in bfloat16 or wider, within the bound.
No kernel may reach another device: no remote copies, remote signals or barrier semaphores. Data moves between devices by JAX's collectives and lax.ppermute only.
A program may use at most 192 MiB of HBM per device.

v0:
```python
import math

import jax
import jax.numpy as jnp
from jax import lax
from jax.sharding import PartitionSpec as P

SAMP = 8


HIGHEST = lax.Precision.HIGHEST
CUBE_OFFSETS = [(a, b, c) for a in range(3) for b in range(3) for c in range(3)]


def entering(value, axis, join, neutral, backward):
    count, mine = (lax.axis_size(axis), lax.axis_index(axis))
    pieces = lax.all_gather(value, axis)
    if backward:
        pieces = pieces[::-1]
        mine = count - 1 - mine
    total = jnp.full_like(value, 0) + jnp.asarray(neutral, value.dtype)

    def hop(position, total):
        longer = join(total, pieces[position])
        return jnp.where(position < mine, longer, total)

    return lax.fori_loop(0, count - 1, hop, total)


def unfold_cells(block_set):
    brick_count = block_set.shape[0]
    channel_width = block_set.shape[1]
    cube = block_set.reshape(brick_count, channel_width, 8, 8, 8)
    padded = jnp.pad(cube, ((0, 0), (0, 0), (1, 1), (1, 1), (1, 1)))
    columns = [
        padded[:, :, a : a + 8, b : b + 8, c : c + 8].reshape(brick_count, channel_width, 512)
        for a, b, c in CUBE_OFFSETS
    ]
    return jnp.stack(columns, axis=1).reshape(brick_count, 27 * channel_width, 512)


def conv_backward(block_set, block_cot, conv_w, conv_b):
    unfolded = unfold_cells(block_set)
    pre_act = (
        jnp.einsum("oc,bcn->obn", conv_w, unfolded, preferred_element_type=jnp.float32)
        + conv_b[:, None, None]
    )
    _, gelu_pull = jax.vjp(jax.nn.gelu, pre_act)
    pre_grad = gelu_pull(block_cot)[0].astype(jnp.bfloat16)
    weight_grad = jnp.einsum("obn,bcn->oc", pre_grad, unfolded, preferred_element_type=jnp.float32)
    bias_grad = jnp.sum(pre_grad.astype(jnp.float32), axis=(1, 2))
    column_grad = jnp.einsum("oc,obn->bcn", conv_w, pre_grad, preferred_element_type=jnp.float32)
    _, fold_pull = jax.vjp(unfold_cells, jnp.zeros(block_set.shape, jnp.float32))
    block_grad = fold_pull(column_grad)[0]
    return (weight_grad, bias_grad, block_grad.astype(jnp.bfloat16))


def field_head(feature_cols, weight_one, bias_one, weight_two):
    hidden = (
        jnp.einsum("ch,cm->hm", weight_one, feature_cols, precision=HIGHEST) + bias_one[:, None]
    )
    outputs = jnp.einsum("hk,hm->km", weight_two, jax.nn.gelu(hidden), precision=HIGHEST)
    return (jax.nn.softplus(outputs[0]), jax.nn.sigmoid(outputs[1]))


def render_terms(density, intensity, depth_grid, step_size):
    optical = density * step_size
    before = jnp.cumsum(optical, axis=-1) - optical
    weights = jnp.exp(-before) * (1.0 - jnp.exp(-optical))
    return (
        jnp.sum(weights * depth_grid, axis=-1),
        jnp.sum(weights * intensity, axis=-1),
        jnp.sum(optical, axis=-1),
    )


def add_terms(first_term, second_term):
    return first_term + second_term


def local(
    bricks,
    conv_w,
    conv_b,
    head_w1,
    head_b1,
    head_w2,
    queries,
    sample_src,
    depth_target,
    inten_target,
    drop_label,
):
    shells = lax.axis_size("shell")
    sectors = lax.axis_size("sector")
    shell_index = lax.axis_index("shell")
    local_bricks = bricks[0]
    brick_count = local_bricks.shape[0]
    channels = local_bricks.shape[1]
    group_size = math.gcd(brick_count, 8)
    group_cols = group_size * 512
    group_total = brick_count // group_size
    weight_one = head_w1.astype(jnp.float32)
    brick_groups = local_bricks.reshape(group_total, group_size, channels, 512)

    def decode_group(group_id, table_now):
        block_set = lax.dynamic_index_in_dim(brick_groups, group_id, 0, keepdims=False)
        pre_act = (
            jnp.einsum(
                "oc,bcn->obn", conv_w, unfold_cells(block_set), preferred_element_type=jnp.float32
            )
            + conv_b[:, None, None]
        )
        values = jax.nn.gelu(pre_act).astype(jnp.bfloat16).reshape(channels, group_cols)
        return values

    cell_table = lax.fori_loop(
        0, group_total, decode_group, jnp.zeros((channels, brick_count * 512), jnp.bfloat16)
    )
    requests = queries[0]
    capacity = requests.shape[1]
    owner_addr = lax.all_to_all(
        requests, "sector", split_axis=0, concat_axis=0, tiled=True
    ).reshape(-1)
    live_slot = owner_addr >= 0
    picked = jnp.take(cell_table, jnp.where(live_slot, owner_addr, 0), axis=1)
    owner_feats = jnp.where(live_slot[None, :], picked, jnp.zeros((), jnp.bfloat16))
    sources = sample_src[0]
    replies = lax.all_to_all(
        owner_feats.reshape(channels, sectors, capacity),
        "sector",
        split_axis=1,
        concat_axis=1,
        tiled=True,
    )
    sample_cols = jnp.take(replies.reshape(channels, sectors * capacity), sources, axis=1).astype(
        jnp.float32
    )
    (density, intensity), head_pull = jax.vjp(field_head, sample_cols, weight_one, head_b1, head_w2)
    ray_count = sources.shape[0] // SAMP
    density = density.reshape(ray_count, SAMP)
    intensity = intensity.reshape(ray_count, SAMP)
    step_size = 2.0 / (shells * SAMP)
    depth_grid = (
        shell_index.astype(jnp.float32) * SAMP + jnp.arange(SAMP, dtype=jnp.float32) + 0.5
    ) / (shells * SAMP)

    def local_render(dens_in, inten_in):
        return render_terms(dens_in, inten_in, depth_grid, step_size)

    (shell_depth, shell_inten, shell_tau), render_pull = jax.vjp(local_render, density, intensity)
    dropped = drop_label.astype(jnp.float32)
    kept_weight = 1.0 - dropped
    zeros_rays = jnp.zeros_like(shell_tau)
    prefix = entering(shell_tau, "shell", add_terms, zeros_rays, False)
    entry_trans = jnp.exp(-prefix)
    ray_depth, ray_inten, tau_total = lax.psum(
        (entry_trans * shell_depth, entry_trans * shell_inten, shell_tau), "shell"
    )
    escape = jnp.exp(-tau_total)
    grad_depth = 2.0 * kept_weight * (ray_depth - depth_target)
    grad_inten = 2.0 * kept_weight * (ray_inten - inten_target)
    own_weight = (grad_depth * shell_depth + grad_inten * shell_inten) * entry_trans
    behind = entering(own_weight, "shell", add_terms, zeros_rays, True)
    grad_escape = 2.0 * (escape - dropped)
    dens_grad, inten_grad = render_pull(
        (grad_depth * entry_trans, grad_inten * entry_trans, -grad_escape * escape - behind)
    )
    ray_loss = jnp.sum(
        kept_weight * ((ray_depth - depth_target) ** 2 + (ray_inten - inten_target) ** 2)
        + (escape - dropped) ** 2
    )
    loss_mean = lax.psum(ray_loss, "sector") / (ray_count * sectors)
    sample_grad, grad_one, grad_bias_one, grad_two = head_pull(
        (dens_grad.reshape(-1), inten_grad.reshape(-1))
    )
    buckets = jnp.zeros((channels, sectors * capacity), jnp.float32).at[:, sources].set(sample_grad)
    owner_grad = lax.all_to_all(
        buckets.reshape(channels, sectors, capacity),
        "sector",
        split_axis=1,
        concat_axis=1,
        tiled=True,
    ).reshape(channels, sectors * capacity)
    target_index = jnp.where(live_slot, owner_addr, brick_count * 512)
    table_grad = (
        jnp.zeros((channels, brick_count * 512), jnp.float32)
        .at[:, target_index]
        .add(owner_grad, mode="drop")
    )

    def conv_back(totals, group_id):
        block_set = lax.dynamic_index_in_dim(brick_groups, group_id, 0, keepdims=False)
        block_cot = table_grad.reshape(channels, group_size, 512)
        weight_grad, bias_grad, block_grad = conv_backward(block_set, block_cot, conv_w, conv_b)
        return ((totals[0] + weight_grad, totals[1] + bias_grad), block_grad)

    start = (jnp.zeros(conv_w.shape, jnp.float32), jnp.zeros_like(conv_b))
    (conv_grad, conv_bias_grad), brick_grads = lax.scan(
        conv_back, start, jnp.arange(group_total, dtype=jnp.int32)
    )
    summed = lax.psum(
        (conv_grad, conv_bias_grad, grad_one, grad_bias_one, grad_two), ("shell", "sector")
    )
    return (
        loss_mean,
        summed[0],
        summed[1],
        summed[2],
        summed[3],
        summed[4],
        brick_grads,
        ray_depth,
    )


def solution(mesh):
    return jax.shard_map(
        local,
        mesh=mesh,
        in_specs=(
            P("shell", "sector", None, None),
            P(),
            P(),
            P(),
            P(),
            P(),
            P("shell", "sector", None),
            P("shell", "sector"),
            P("sector"),
            P("sector"),
            P("sector"),
        ),
        out_specs=(P(), P(), P(), P(), P(), P(), P("shell", "sector", None, None), P("sector")),
        check_vma=False,
    )
```

profile of v0, /device:TPU:1, one launch (start us, length us, event | category | flops | bytes accessed | tf_op | source)
XLA Modules:
  0.0 665.0 jit_solution(13087959850178110753)
XLA Ops:
  8.6 8.6 %all-to-all-start = ((s32[32,1,256]{2,1,0:T(1,128)}), s32[32,1,256]{2,1,0:T(1,128)S(1)}, u32[]{:S(2)}, u32[]{:S(2)}) async-start(s32[32,1,256]{2,1,0:T(1,128)} %all_to_all.12), calls=%async_computation | async-start | bytes 65536 | tf_op jit(solution)/shard_map/all_to_all | solution.py:122
  18.6 3.4 pad_slice_fusion.1
  22.1 6.8 %pad_slice_fusion = (bf16[8,32,8,8,8]{1,4,3,2,0:T(8,128)(2,1)}, bf16[8,32,8,8,8]{1,4,3,2,0:T(8,128)(2,1)}, bf16[8,32,8,8,8]{1,4,3,2,0:T(8,128)(2,1)}, bf16[8,32,...) fusion(bf16[8,32,8,8,8]{1,4,3,2,0:T(8,128)(2,1)S(1)} %bitcast.139), kind=kLoop, calls=%fused_computation.8 | loop fusion | bytes 5242880 | tf_op jit(solution)/shard_map/while/body/eval_jaxpr/slice | solution.py:36
  28.9 2.3 copy.147
  31.3 2.2 copy.142
  33.5 2.3 copy.143
  38.0 2.3 copy.145
  40.3 2.3 copy.146
  43.6 2.4 copy.148
  54.9 2.3 copy.128
  57.2 2.2 copy.129
  59.4 2.2 copy.130
  61.7 2.3 copy.131
  67.2 2.3 copy.134
  69.6 2.2 copy.135
  92.7 2.3 copy.136
  95.0 2.3 copy.137
  97.2 2.2 copy.138
  118.1 5.1 multiply_convert_fusion
  124.4 24.0 %gather_fusion = bf16[8192,32]{1,0:T(8,128)(2,1)S(1)} fusion(bf16[32,4096]{0,1:T(8,128)(2,1)S(1)} %bitcast.136, s32[8192]{0:T(1024)S(1)} %broadcast_clamp_fusion), kind=kCustom, calls=%fused_computation | custom fusion | bytes 1081344 | tf_op jit(solution)/shard_map/jit(_take)/gather | solution.py:126
  150.3 7.4 %all-to-all-start.1 = ((bf16[32,32,256]{2,0,1:T(8,128)(2,1)}), bf16[32,32,256]{2,0,1:T(8,128)(2,1)S(1)}, u32[]{:S(2)}, u32[]{:S(2)}) async-start(bf16[32,32,256]{2,0,1:T(8,128)(2,1)} %select_select_fusion), calls=%async_computation.1 | async-start | bytes 1048576 | tf_op jit(solution)/shard_map/all_to_all | solution.py:129
  157.8 11.5 %all-to-all-done.1 = bf16[32,32,256]{2,0,1:T(8,128)(2,1)S(1)} async-done(((bf16[32,32,256]{2,0,1:T(8,128)(2,1)}), bf16[32,32,256]{2,0,1:T(8,128)(2,1)S(1)}, u32[]{:S(2)}, u32[]{:S(2)}) %all-to-all-start.1) | async-done | bytes 524320 | tf_op jit(solution)/shard_map/all_to_all | solution.py:129
  170.4 12.1 %gather_fusion.1 = bf16[4096,32]{1,0:T(8,128)(2,1)S(1)} fusion(bf16[32,8192]{0,1:T(8,128)(2,1)S(1)} %bitcast.163, s32[4096]{0:T(1024)S(1)} %broadcast_clamp_fusion.1), kind=kCustom, calls=%fused_computation.1 | custom fusion | bytes 540672 | tf_op jit(solution)/shard_map/jit(_take)/gather | solution.py:136
  187.0 19.6 %all-gather.2 = f32[8,1,512]{2,1,0:T(1,128)S(1)} all-gather(f32[1,1,512]{2,1,0:T(1,128)S(1)} %bitcast.209), channel_id=2, replica_groups=mesh['shell'=8,'sector'=32] {'shell'}, dimensions={0}, use_global_device_ids=true | all-gather | bytes 18432 | tf_op jit(solution)/shard_map/all_gather | solution.py:17
  207.0 11.4 %all-reduce.31 = (f32[512]{0:T(512)S(1)}, f32[512]{0:T(512)S(1)}, f32[512]{0:T(512)S(1)}) all-reduce(f32[512]{0:T(512)S(1)} %get-tuple-element.265, f32[512]{0:T(512)S(1)} %get-tuple-element.360, f32[512]{0:T(512)S(1)} %get-tuple-element.359), channel_id=1, replica_groups=mesh['shell'=8,'sector'=32] {'shell'}, use_global_device_ids=true, to_apply=%region_8.9 | all-reduce | flops 1536 | bytes 12288 | tf_op jit(solution)/shard_map/psum | solution.py:157
  220.8 15.9 %all-gather.3 = f32[8,1,512]{2,1,0:T(1,128)S(1)} all-gather(f32[1,1,512]{2,1,0:T(1,128)} %bitcast.210), channel_id=3, replica_groups=mesh['shell'=8,'sector'=32] {'shell'}, dimensions={0}, use_global_device_ids=true | all-gather | bytes 18432 | tf_op jit(solution)/shard_map/all_gather | solution.py:17
  239.9 2.4 fusion.56
  242.3 3.9 fusion.57
  246.2 13.2 %scatter_custom_fusion = f32[32,8192]{0,1:T(8,128)} fusion(s32[4096]{0:T(1024)S(1)} %bitcast.205, f32[4096,32]{1,0:T(8,128)} %fusion.57, f32[]{:T(128)} %constant.164.clone.1), kind=kCustom, calls=%fused_computation.45 | custom fusion | bytes 1049088 | tf_op jit(solution)/shard_map/scatter | solution.py:177
  259.5 3.6 copy.154
  263.1 18.7 %all-to-all-start.2 = ((f32[32,32,256]{2,0,1:T(8,128)}), f32[32,32,256]{2,0,1:T(8,128)S(1)}, u32[]{:S(2)}, u32[]{:S(2)}) async-start(f32[32,32,256]{2,0,1:T(8,128)} %copy.154), calls=%async_computation.2 | async-start | bytes 2097152 | tf_op jit(solution)/shard_map/all_to_all | solution.py:178
  281.8 71.8 %psum.66 = f32[]{:T(128)} all-reduce(f32[]{:T(128)} %get-tuple-element.354), channel_id=1, replica_groups=mesh['shell'=8,'sector'=32] {'sector'}, use_global_device_ids=true, to_apply=%region_10.11 | all-reduce | flops 1 | bytes 8 | tf_op jit(solution)/shard_map/psum | solution.py:173
  354.2 2.4 fusion.20
  358.3 2.8 copy.156
  361.1 45.0 %scatter_custom_fusion.1 = f32[32,4096]{0,1:T(8,128)S(1)} fusion(s32[8192]{0:T(1024)} %bitcast.208, f32[8192,32]{1,0:T(8,128)} %copy.156, f32[]{:T(128)} %constant.164.clone.1), kind=kCustom, calls=%fused_computation.58 | custom fusion | flops 262144 | bytes 524800 | tf_op jit(solution)/shard_map/scatter-add | solution.py:189
  407.2 5.8 convolution_bitcast_fusion.2
  417.1 3.4 fusion.54
  422.1 3.0 copy.197
  425.1 3.0 copy.204
  428.1 3.0 copy.203
  431.0 3.0 copy.202
  434.0 3.0 copy.201
  437.0 3.0 copy.200
  440.0 3.0 copy.199
  443.0 3.0 copy.223
  445.9 3.0 copy.222
  448.9 3.0 copy.221
  451.9 3.0 copy.220
  454.9 3.0 copy.219
  457.9 3.0 copy.218
  460.9 3.0 copy.217
  463.9 3.0 copy.216
  466.9 3.0 copy.215
  469.8 3.0 copy.214
  472.8 3.0 copy.213
  475.9 3.0 copy.212
  478.8 3.0 copy.211
  481.8 3.0 copy.210
  484.8 3.0 copy.209
  487.8 3.0 copy.208
  490.8 3.2 copy.207
  497.9 16.8 %pad_add_fusion = f32[8,32,10,10,10]{1,4,3,2,0:T(8,128)S(1)} fusion(f32[8,32,8,8,8]{1,4,3,2,0:T(8,128)} %bitcast.148, f32[8,32,8,8,8]{1,4,3,2,0:T(8,128)} %bitcast.149, f32[8,32,8,8,8]{1,4,3,2,0:T(8,128)} %bitcast.150, f32[8,32,8,8,8]{1,4,3,2,0:T(8,128)} %bitcast.151, f32[8,32,8,8,8]{1,4,3,2,0:T(8,128)} %bitcast.152, f32[8,32,8,8,8]{1,4,3,2,0:T(8,128)} %bitcast.153, ...), kind=kLoop, calls=%fused_computation.34 | loop fusion | flops 5376000 | bytes 12558336 | tf_op jit(solution)/shard_map/while/body/eval_jaxpr/transpose(jvp())/add_any | solution.py:36
  515.8 72.8 %all-reduce.30 = (f32[32]{0:T(128)}, f32[32,64]{1,0:T(8,128)}, f32[64]{0:T(128)}, f32[64,2]{0,1:T(2,128)}) all-reduce(f32[32]{0:T(128)S(1)} %get-tuple-element.289, f32[32,64]{1,0:T(8,128)S(1)} %fusion.21, f32[64]{0:T(128)S(1)} %get-tuple-element.363, f32[64,2]{0,1:T(2,128)S(1)} %fusion.20), channel_id=1, replica_groups=mesh['shell'=8,'sector'=32] {'shell','sector'}, use_global_device_ids=true, to_apply=%region_18.19 | all-reduce | flops 2272 | bytes 18176 | tf_op jit(solution)/shard_map/psum | solution.py:202
  589.7 65.3 %all-reduce.34.cloned.1.call-done = f32[32,864]{1,0:T(8,128)} async-done(((f32[32,864]{1,0:T(8,128)}), f32[32,864]{1,0:T(8,128)}) %all-reduce.34.cloned.1.call-update) | async-done | bytes 110608 | tf_op jit(solution)/shard_map/psum | solution.py:202
  (184 shorter events, 88.6 us)
Async XLA Ops:
  7.2 110.9 %copy-start = (bf16[32,864]{1,0:T(8,128)(2,1)S(1)}, bf16[32,864]{1,0:T(8,128)(2,1)}, u32[]{:S(2)}) copy-start(bf16[32,864]{1,0:T(8,128)(2,1)} %param.16) | copy-start | bytes 165892
  8.6 115.1 %all-to-all-start = ((s32[32,1,256]{2,1,0:T(1,128)}), s32[32,1,256]{2,1,0:T(1,128)S(1)}, u32[]{:S(2)}, u32[]{:S(2)}) async-start(s32[32,1,256]{2,1,0:T(1,128)} %all_to_all.12), calls=%async_computation | async-start | bytes 65536 | tf_op jit(solution)/shard_map/all_to_all | solution.py:122
  22.1 6.8 %copy-start.18 = (s32[1,4096]{1,0:T(1,128)S(1)}, s32[1,4096]{1,0:T(1,128)}, u32[]{:S(2)}) copy-start(s32[1,4096]{1,0:T(1,128)} %param.22) | copy-start | bytes 49156
  28.9 13.6 %copy-start.9 = (bf16[8,32,8,8,8]{1,4,3,2,0:T(8,128)(2,1)S(1)}, bf16[8,32,8,8,8]{1,4,3,2,0:T(8,128)(2,1)}, u32[]{:S(2)}) copy-start(bf16[8,32,8,8,8]{1,4,3,2,0:T(8,128)(2,1)} %get-tuple-element.345) | copy-start | bytes 786436
  43.6 22.6 %copy-start.8 = (bf16[8,32,8,8,8]{1,4,3,2,0:T(8,128)(2,1)S(1)}, bf16[8,32,8,8,8]{1,4,3,2,0:T(8,128)(2,1)}, u32[]{:S(2)}) copy-start(bf16[8,32,8,8,8]{1,4,3,2,0:T(8,128)(2,1)} %get-tuple-element.330) | copy-start | bytes 786436
  61.7 30.3 %copy-start.12 = (bf16[1,8,32,512]{3,2,1,0:T(8,128)(2,1)S(1)}, bf16[1,8,32,512]{3,2,1,0:T(8,128)(2,1)}, u32[]{:S(2)}) copy-start(bf16[1,8,32,512]{3,2,1,0:T(8,128)(2,1)} %param.15) | copy-start | bytes 786436
  67.2 32.2 %copy-start.7 = (bf16[8,32,8,8,8]{1,4,3,2,0:T(8,128)(2,1)S(1)}, bf16[8,32,8,8,8]{1,4,3,2,0:T(8,128)(2,1)}, u32[]{:S(2)}) copy-start(bf16[8,32,8,8,8]{1,4,3,2,0:T(8,128)(2,1)} %get-tuple-element.336) | copy-start | bytes 786436
  92.7 23.9 %copy-start.13 = (bf16[8,1,32,512]{3,2,1,0:T(8,128)(2,1)S(1)}, bf16[8,1,32,512]{3,2,1,0:T(8,128)(2,1)}, u32[]{:S(2)}) copy-start(bf16[8,1,32,512]{3,2,1,0:T(8,128)(2,1)} %copy.147) | copy-start | bytes 786436
  95.0 23.1 %copy-start.27 = (f32[32]{0:T(128)S(1)}, f32[32]{0:T(128)}, u32[]{:S(2)}) copy-start(f32[32]{0:T(128)} %param.17) | copy-start | bytes 388
  100.5 13.9 %copy-start.17 = (bf16[8,1,32,512]{3,2,1,0:T(8,128)(2,1)S(1)}, bf16[8,1,32,512]{3,2,1,0:T(8,128)(2,1)}, u32[]{:S(2)}) copy-start(bf16[8,1,32,512]{3,2,1,0:T(8,128)(2,1)} %copy.144) | copy-start | bytes 786436
  100.5 14.6 %copy-start.15 = (bf16[8,1,32,512]{3,2,1,0:T(8,128)(2,1)S(1)}, bf16[8,1,32,512]{3,2,1,0:T(8,128)(2,1)}, u32[]{:S(2)}) copy-start(bf16[8,1,32,512]{3,2,1,0:T(8,128)(2,1)} %copy.145) | copy-start | bytes 786436
  100.5 15.3 %copy-start.14 = (bf16[8,1,32,512]{3,2,1,0:T(8,128)(2,1)S(1)}, bf16[8,1,32,512]{3,2,1,0:T(8,128)(2,1)}, u32[]{:S(2)}) copy-start(bf16[8,1,32,512]{3,2,1,0:T(8,128)(2,1)} %copy.146) | copy-start | bytes 786436
  100.5 16.8 %copy-start.16 = (bf16[8,1,32,512]{3,2,1,0:T(8,128)(2,1)S(1)}, bf16[8,1,32,512]{3,2,1,0:T(8,128)(2,1)}, u32[]{:S(2)}) copy-start(bf16[8,1,32,512]{3,2,1,0:T(8,128)(2,1)} %copy.148) | copy-start | bytes 786436
  124.4 58.2 %copy-start.19 = (bf16[32,64]{1,0:T(8,128)(2,1)S(1)}, bf16[32,64]{1,0:T(8,128)(2,1)}, u32[]{:S(2)}) copy-start(bf16[32,64]{1,0:T(8,128)(2,1)} %param.18) | copy-start | bytes 12292
  124.4 58.2 %copy-start.28 = (f32[64]{0:T(128)S(1)}, f32[64]{0:T(128)}, u32[]{:S(2)}) copy-start(f32[64]{0:T(128)} %param.19) | copy-start | bytes 772
  148.4 35.0 %copy-start.29 = (f32[64,2]{0,1:T(2,128)S(1)}, f32[64,2]{0,1:T(2,128)}, u32[]{:S(2)}) copy-start(f32[64,2]{0,1:T(2,128)} %param.20) | copy-start | bytes 1540
  150.3 19.0 %all-to-all-start.1 = ((bf16[32,32,256]{2,0,1:T(8,128)(2,1)}), bf16[32,32,256]{2,0,1:T(8,128)(2,1)S(1)}, u32[]{:S(2)}, u32[]{:S(2)}) async-start(bf16[32,32,256]{2,0,1:T(8,128)(2,1)} %select_select_fusion), calls=%async_computation.1 | async-start | bytes 1048576 | tf_op jit(solution)/shard_map/all_to_all | solution.py:129
  157.7 48.9 %copy-start.26 = (f32[8]{0:T(128)}, f32[8]{0:T(128)S(1)}, u32[]{:S(2)}) copy-start(f32[8]{0:T(128)S(1)} %add_multiply_fusion.1) | copy-start | bytes 100
  157.8 60.7 %copy-start.21 = (s32[512]{0:T(512)S(1)}, s32[512]{0:T(512)}, u32[]{:S(2)}) copy-start(s32[512]{0:T(512)} %param.25) | copy-start | bytes 6148
  157.8 60.7 %copy-start.23 = (f32[512]{0:T(512)S(1)}, f32[512]{0:T(512)}, u32[]{:S(2)}) copy-start(f32[512]{0:T(512)} %param.24) | copy-start | bytes 6148
  157.8 60.7 %copy-start.24 = (f32[512]{0:T(512)S(1)}, f32[512]{0:T(512)}, u32[]{:S(2)}) copy-start(f32[512]{0:T(512)} %param.23) | copy-start | bytes 6148
  183.4 58.9 %copy-start.11 = (f32[64,4096]{1,0:T(8,128)}, f32[64,4096]{1,0:T(8,128)S(1)}, u32[]{:S(2)}) copy-start(f32[64,4096]{1,0:T(8,128)S(1)} %fusion) | copy-start | bytes 3145732
  218.4 1.2 copy-start.22
  218.5 1.2 copy-start.25
  219.7 0.9 copy-start.20
  263.1 95.2 %all-to-all-start.2 = ((f32[32,32,256]{2,0,1:T(8,128)}), f32[32,32,256]{2,0,1:T(8,128)S(1)}, u32[]{:S(2)}, u32[]{:S(2)}) async-start(f32[32,32,256]{2,0,1:T(8,128)} %copy.154), calls=%async_computation.2 | async-start | bytes 2097152 | tf_op jit(solution)/shard_map/all_to_all | solution.py:178
  281.7 373.3 %all-reduce.34.cloned.1.call-start = ((), (), s32[]{:S(2)}) async-start(), calls=%async_computation.3 | async-start | bytes 229376 | tf_op jit(solution)/shard_map/psum | solution.py:202
  358.2 48.5 %copy-start.10 = (f32[32,8,512]{2,0,1:T(8,128)S(1)}, f32[32,8,512]{2,0,1:T(8,128)}, u32[]{:S(2)}) copy-start(f32[32,8,512]{2,0,1:T(8,128)} %get-tuple-element.362) | copy-start | bytes 1572868
  497.9 16.8 %copy-start.2 = (f32[8,1,32,512]{2,3,0,1:T(8,128)S(1)}, f32[8,1,32,512]{2,3,0,1:T(8,128)}, u32[]{:S(2)}) copy-start(f32[8,1,32,512]{2,3,0,1:T(8,128)} %copy.223) | copy-start | bytes 1572868
  497.9 16.8 %copy-start.3 = (f32[8,1,32,512]{2,3,0,1:T(8,128)S(1)}, f32[8,1,32,512]{2,3,0,1:T(8,128)}, u32[]{:S(2)}) copy-start(f32[8,1,32,512]{2,3,0,1:T(8,128)} %copy.222) | copy-start | bytes 1572868
  497.9 16.8 %copy-start.4 = (f32[8,1,32,512]{2,3,0,1:T(8,128)S(1)}, f32[8,1,32,512]{2,3,0,1:T(8,128)}, u32[]{:S(2)}) copy-start(f32[8,1,32,512]{2,3,0,1:T(8,128)} %copy.221) | copy-start | bytes 1572868
  497.9 16.8 %copy-start.5 = (f32[8,1,32,512]{2,3,0,1:T(8,128)S(1)}, f32[8,1,32,512]{2,3,0,1:T(8,128)}, u32[]{:S(2)}) copy-start(f32[8,1,32,512]{2,3,0,1:T(8,128)} %copy.220) | copy-start | bytes 1572868
  497.9 16.8 %copy-start.6 = (f32[8,1,32,512]{2,3,0,1:T(8,128)S(1)}, f32[8,1,32,512]{2,3,0,1:T(8,128)}, u32[]{:S(2)}) copy-start(f32[8,1,32,512]{2,3,0,1:T(8,128)} %copy.219) | copy-start | bytes 1572868
  514.7 141.9 %copy-start.1 = (bf16[32,864]{1,0:T(8,128)(2,1)S(1)}, bf16[32,864]{1,0:T(8,128)(2,1)}, u32[]{:S(2)}) copy-start(bf16[32,864]{1,0:T(8,128)(2,1)} %param.16) | copy-start | bytes 165892
Sparse Core Ops, SparseCore 0:
  420.6 234.3 all-reduce.33
where the time goes:
time: 677 us; the launch traced here: 665 us
  local copies, waits for them, and re-layouts  249 us (37%)
  blocking collectives  192 us (28%)
  waiting for transfers between devices  76.9 us (11%)
  other arithmetic  70.1 us (10%)
  starting transfers between devices  34.7 us (5%)
  matrix products  25.1 us (4%)
  between operations  16.9 us (2%)
    unnamed x118, local copies, waits for them, and re-layouts  119 us
    psum x1, blocking collectives, local(): lax.psum((conv_grad, conv_bias_grad, grad_one, grad_bias_one, grad_two),...  72.8 us
    psum x1, blocking collectives, local(): loss_mean = lax.psum(ray_loss, 'sector') / (ray_count * sectors)  71.8 us
    psum x1, waiting for transfers between devices, local(): lax.psum((conv_grad, conv_bias_grad, grad_one, grad_bias_one, grad_two),...  65.3 us
    reshape x26, local copies, waits for them, and re-layouts, unfold_cells(): jnp.stack(columns, axis=1).reshape(brick_count, 27 * channel_width, 512)  51.4 us
    scatter-add x1, other arithmetic, local(): table_grad = jnp.zeros((channels, brick_count * 512), jnp.float32).at[:,...  45 us
    all_gather x2, blocking collectives, entering(): pieces = lax.all_gather(value, axis)  35.6 us
    gather x2, local copies, waits for them, and re-layouts, local(): picked = jnp.take(cell_table, jnp.where(live_slot, owner_addr, 0), axis=1)  25 us
  transfers between devices with their start and end apart: 4, of which 2 were waited for; matrix products, arithmetic and copies ran while one was open for 31% of the time, Pallas kernels for 0%

commit v1 on v0

v1 whole, which is shorter than its diff:
```python
import functools

import jax
import jax.numpy as jnp
from jax import lax
from jax.experimental import pallas as pl
from jax.experimental.pallas import tpu as pltpu
from jax.sharding import PartitionSpec as P

SAMP = 8
CELLS = 512
LANE = 128
HI = 256
GELU_C = 0.7978845608028654
GELU_A = 0.044715

F32 = jnp.float32
BF16 = jnp.bfloat16
NT = (((1,), (1,)), ((), ()))
TN = (((0,), (0,)), ((), ()))
NN = (((1,), (0,)), ((), ()))


def dot(a, b, dims=NN):
    return lax.dot_general(a, b, dims, preferred_element_type=F32)


def iota(shape, axis):
    return lax.broadcasted_iota(jnp.int32, shape, axis)


def gelu_pair(x):
    x2 = x * x
    t = jnp.tanh(GELU_C * (x + GELU_A * (x2 * x)))
    half = 0.5 * (1.0 + t)
    slope = half + 0.5 * x * (1.0 - t * t) * (GELU_C * (1.0 + 3.0 * GELU_A * x2))
    return x * half, slope


def split3(v):
    a = v.astype(BF16).astype(F32)
    r = v - a
    b = r.astype(BF16).astype(F32)
    c = (r - b).astype(BF16).astype(F32)
    return a, b, c


def split2(v):
    a = v.astype(BF16)
    return a, (v - a.astype(F32)).astype(BF16)


def column(row):
    n = row.shape[1]
    eye = iota((n, n), 0) == iota((n, n), 1)
    return jnp.sum(jnp.where(eye, row, 0.0), axis=1, keepdims=True)


def row_of(col):
    n = col.shape[0]
    eye = iota((n, n), 0) == iota((n, n), 1)
    return jnp.sum(jnp.where(eye, col, 0.0), axis=0, keepdims=True)


def moved(x, step):
    return pltpu.roll(x, (-step) % x.shape[1], 1)


def shift_cells(x, direction, stride):
    if direction == 0:
        return x
    pos = (iota((1, CELLS), 1) // stride) & 7
    ok = (pos >= 1) if direction < 0 else (pos <= 6)
    return jnp.where(ok, moved(x, direction * stride), 0.0)


def c_columns(block):
    wide = block.astype(F32)
    return jnp.concatenate([shift_cells(wide, c - 1, 1) for c in range(3)], axis=0).astype(BF16)


def ab_columns(cot):
    parts = []
    for a in range(3):
        part = shift_cells(cot, 1 - a, 64)
        for b in range(3):
            parts.append(shift_cells(part, 1 - b, 8))
    return jnp.concatenate(parts, axis=0).astype(BF16)


def decode_kernel(bricks, wf, conv_b, w1, b1, w2, dec_out, slope_out, planes_out, factor_out, e0_s, e1_s):
    count, ch = bricks.shape[0], bricks.shape[1]
    bias = column(conv_b[...])
    bias1 = column(b1[...])
    for n in range(count):
        y = dot(wf[...], c_columns(bricks[n]))
        pre = bias
        for a in range(3):
            rows = [y[(3 * a + b) * ch : (3 * a + b + 1) * ch] for b in range(3)]
            t = rows[1] + shift_cells(rows[0], -1, 8) + shift_cells(rows[2], 1, 8)
            pre = pre + shift_cells(t, a - 1, 64)
        value, slope = gelu_pair(pre)
        dec = value.astype(BF16)
        dec_out[:, n * CELLS : (n + 1) * CELLS] = dec
        slope_out[:, n * CELLS : (n + 1) * CELLS] = slope
        h = dot(w1[...], dec, TN) + bias1
        g, _ = gelu_pair(h)
        e0 = jnp.sum(w2[:, 0:1] * g, axis=0, keepdims=True)
        e1 = jnp.sum(w2[:, 1:2] * g, axis=0, keepdims=True)
        for half in range(CELLS // HI):
            at = n * (CELLS // HI) + half
            e0_s[at : at + 1, :] = e0[:, half * HI : (half + 1) * HI]
            e1_s[at : at + 1, :] = e1[:, half * HI : (half + 1) * HI]
    e0 = e0_s[...]
    e1 = e1_s[...]
    density = jnp.maximum(e0, 0.0) + jnp.log1p(jnp.exp(-jnp.abs(e0)))
    intensity = 1.0 / (1.0 + jnp.exp(-e1))
    factor_out[0] = 1.0 / (1.0 + jnp.exp(-e0))
    factor_out[1] = intensity * (1.0 - intensity)
    planes_out[...] = jnp.concatenate(split3(density) + split3(intensity), axis=0).astype(BF16)


def one_hot(low):
    return jnp.where(iota((HI, low.shape[1]), 0) == low, 1.0, 0.0).astype(BF16)


def pick(planes, groups, address):
    found = dot(planes, one_hot(address & (HI - 1)))
    mine = iota((groups, address.shape[1]), 0) == (address >> 8)
    out = []
    for v in range(2):
        p = [found[(3 * v + k) * groups : (3 * v + k + 1) * groups] for k in range(3)]
        out.append(jnp.sum(jnp.where(mine, (p[0] + p[1]) + p[2], 0.0), axis=0, keepdims=True))
    return out


def spread(rows, groups, address):
    mine = iota((groups, address.shape[1]), 0) == (address >> 8)
    stack = jnp.concatenate([jnp.where(mine, r, 0.0) for r in rows], axis=0).astype(BF16)
    return dot(stack, one_hot(address & (HI - 1)), NT)


def join_planes(acc, groups):
    out = []
    for v in range(2):
        p = [acc[(3 * v + k) * groups : (3 * v + k + 1) * groups] for k in range(3)]
        out.append((p[0] + p[1]) + p[2])
    return out


def owner_pick_kernel(addr, planes, out):
    groups = planes.shape[0] // 6

    def body(s, carry):
        pair = pick(planes[...], groups, addr[pl.ds(s, 1), :])
        for v in range(2):
            for half in range(2):
                out[s, 2 * v + half : 2 * v + half + 1, :] = pair[v][:, half * LANE : (half + 1) * LANE]
        return carry

    lax.fori_loop(0, addr.shape[0], body, 0, unroll=4)


def excl_down(x):
    n = x.shape[0]
    at = iota(x.shape, 0)
    acc = jnp.where(at >= 1, pltpu.roll(x, 1, 0), 0.0)
    step = 1
    while step < n:
        acc = acc + jnp.where(at >= step, pltpu.roll(acc, step, 0), 0.0)
        step *= 2
    return acc


def excl_up(x):
    n = x.shape[0]
    at = iota(x.shape, 0)
    acc = jnp.where(at < n - 1, pltpu.roll(x, n - 1, 0), 0.0)
    step = 1
    while step < n:
        acc = acc + jnp.where(at < n - step, pltpu.roll(acc, n - step, 0), 0.0)
        step *= 2
    return acc


def sample_depths(shape, shell, shells):
    k = iota(shape, 0).astype(F32)
    return (shell.astype(F32) * SAMP + k + 0.5) / (shells * SAMP)


def sample_kernel(shells, shell_ref, replies, slots, density_out, intensity_out, out):
    groups = replies.shape[0]
    tables = [
        jnp.concatenate([replies[:, 2 * v, :], replies[:, 2 * v + 1, :]], axis=1) for v in range(2)
    ]
    planes = jnp.concatenate(split3(tables[0]) + split3(tables[1]), axis=0).astype(BF16)
    for k in range(SAMP):
        pair = pick(planes, groups, slots[k : k + 1, :])
        density_out[k : k + 1, :] = pair[0]
        intensity_out[k : k + 1, :] = pair[1]
    density = density_out[...]
    optical = density * (2.0 / (shells * SAMP))
    weights = jnp.exp(-excl_down(optical)) * (1.0 - jnp.exp(-optical))
    depth = jnp.sum(weights * sample_depths(density.shape, shell_ref[0], shells), axis=0, keepdims=True)
    inten = jnp.sum(weights * intensity_out[...], axis=0, keepdims=True)
    tau = jnp.sum(optical, axis=0, keepdims=True)
    packed = jnp.concatenate([depth, inten, tau, jnp.zeros_like(tau)], axis=0)
    for s in range(shells):
        out[s] = packed


def render_kernel(
    shells, shell_ref, terms, density, intensity, slots, target, inten_target, drop, buckets_out, depth_out, loss_out
):
    shell = shell_ref[0]
    delta = 2.0 / (shells * SAMP)
    d_all = terms[:, 0, :]
    i_all = terms[:, 1, :]
    t_all = terms[:, 2, :]
    entry = jnp.exp(-excl_down(t_all))
    ray_depth = jnp.sum(entry * d_all, axis=0, keepdims=True)
    ray_inten = jnp.sum(entry * i_all, axis=0, keepdims=True)
    escape = jnp.exp(-jnp.sum(t_all, axis=0, keepdims=True))
    dropped = drop[...].astype(F32)
    kept = 1.0 - dropped
    depth_err = ray_depth - target[...]
    inten_err = ray_inten - inten_target[...]
    loss = kept * (depth_err * depth_err + inten_err * inten_err) + (escape - dropped) * (escape - dropped)
    loss_out[...] = jnp.where(shell == 0, jnp.sum(loss, axis=1, keepdims=True), 0.0)
    depth_out[...] = ray_depth
    grad_depth = 2.0 * kept * depth_err
    grad_inten = 2.0 * kept * inten_err
    own = (grad_depth * d_all + grad_inten * i_all) * entry
    at = iota(own.shape, 0)
    behind = jnp.sum(jnp.where(at > shell, own, 0.0), axis=0, keepdims=True)
    entry_me = jnp.sum(jnp.where(at == shell, entry, 0.0), axis=0, keepdims=True)
    grad_tau = -2.0 * (escape - dropped) * escape - behind
    gd = grad_depth * entry_me
    gi = grad_inten * entry_me
    optical = density[...] * delta
    before = jnp.exp(-excl_down(optical))
    through = jnp.exp(-optical)
    weights = before * (1.0 - through)
    pull = gd * sample_depths(optical.shape, shell, shells) + gi * intensity[...]
    dens_grad = delta * (pull * before * through - excl_up(pull * weights) + grad_tau)
    inten_grad = gi * weights
    planes = split3(dens_grad) + split3(inten_grad)
    groups = buckets_out.shape[0]
    acc = jnp.zeros((6 * groups, HI), F32)
    for k in range(SAMP):
        acc = acc + spread([p[k : k + 1, :] for p in planes], groups, slots[k : k + 1, :])
    pair = join_planes(acc, groups)
    for v in range(2):
        for half in range(2):
            buckets_out[:, 2 * v + half, :] = pair[v][:, half * LANE : (half + 1) * LANE]


def fold_lanes(x):
    total = x[:, 0:LANE]
    for k in range(1, x.shape[1] // LANE):
        total = total + x[:, k * LANE : (k + 1) * LANE]
    return total


def owner_back_kernel(
    addr, cots, factor, dec, slope, bricks, w1, b1, w2, loss, payload_out, cot_out, plane_s
):
    count, ch = bricks.shape[0], bricks.shape[1]
    hid = w1.shape[1]
    groups = factor.shape[1]
    sectors = addr.shape[0]
    for v in range(2):
        whole = jnp.concatenate([cots[:, 2 * v, :], cots[:, 2 * v + 1, :]], axis=1)
        for k, part in enumerate(split3(whole)):
            plane_s[3 * v + k] = part

    def body(s, acc):
        rows = [plane_s[k, pl.ds(s, 1), :] for k in range(6)]
        return acc + spread(rows, groups, addr[pl.ds(s, 1), :])

    acc = lax.fori_loop(0, sectors, body, jnp.zeros((6 * groups, HI), F32), unroll=4)
    pair = join_planes(acc, groups)
    ge = [pair[v] * factor[v] for v in range(2)]
    bias1 = column(b1[...])
    w2_0, w2_1 = w2[:, 0:1], w2[:, 1:2]
    per = CELLS // HI
    acc_w1 = jnp.zeros((ch, hid), F32)
    acc_b1 = jnp.zeros((hid, LANE), F32)
    acc_w20 = jnp.zeros((hid, LANE), F32)
    acc_w21 = jnp.zeros((hid, LANE), F32)
    acc_cb = jnp.zeros((ch, LANE), F32)
    acc_cw = jnp.zeros((9 * ch, 3 * ch), F32)
    for n in range(count):
        cells = slice(n * CELLS, (n + 1) * CELLS)
        rows = [
            jnp.concatenate([ge[v][n * per + k : n * per + k + 1] for k in range(per)], axis=1)
            for v in range(2)
        ]
        dec_n = dec[:, cells]
        g, gs = gelu_pair(dot(w1[...], dec_n, TN) + bias1)
        dh = (w2_0 * rows[0] + w2_1 * rows[1]) * gs
        acc_b1 = acc_b1 + fold_lanes(dh)
        acc_w20 = acc_w20 + fold_lanes(g * rows[0])
        acc_w21 = acc_w21 + fold_lanes(g * rows[1])
        dh_a, dh_b = split2(dh)
        acc_w1 = acc_w1 + (dot(dec_n, dh_a, NT) + dot(dec_n, dh_b, NT))
        df = dot(w1[...], dh_a) + dot(w1[...], dh_b)
        cot = (df * slope[:, cells]).astype(BF16)
        cot_out[:, cells] = cot
        wide = cot.astype(F32)
        acc_cb = acc_cb + fold_lanes(wide)
        acc_cw = acc_cw + dot(ab_columns(wide), c_columns(bricks[n]), NT)
    lane = iota((ch, LANE), 1)
    tiles = [jnp.zeros((ch, LANE), F32) for _ in range(7)]
    pad = jnp.zeros((ch, LANE - 3 * ch), F32)
    for ab in range(9):
        block = jnp.concatenate([acc_cw[ab * ch : (ab + 1) * ch], pad], axis=1)
        tile, off = divmod(3 * ch * ab, LANE)
        if off == 0:
            tiles[tile] = tiles[tile] + block
        else:
            turned = pltpu.roll(block, off, 1)
            tiles[tile] = tiles[tile] + jnp.where(lane >= off, turned, 0.0)
            if tile + 1 < 7:
                tiles[tile + 1] = tiles[tile + 1] + jnp.where(lane < off, turned, 0.0)
    for k in range(7):
        payload_out[:, k, :] = tiles[k]
    small = [
        row_of(jnp.sum(acc_b1, axis=1, keepdims=True)),
        row_of(jnp.sum(acc_w20, axis=1, keepdims=True)),
        row_of(jnp.sum(acc_w21, axis=1, keepdims=True)),
        jnp.concatenate(
            [row_of(jnp.sum(acc_cb, axis=1, keepdims=True)), jnp.zeros((1, hid - ch), F32)], axis=1
        ),
        jnp.broadcast_to(loss[...], (1, hid)),
        jnp.zeros((ch - 5, hid), F32),
    ]
    payload_out[:, 7, :] = jnp.concatenate([acc_w1, jnp.concatenate(small, axis=0)], axis=1)


def bricks_back_kernel(cot, wf, out):
    count, ch = out.shape[0], out.shape[1]
    for n in range(count):
        wide = cot[:, n * CELLS : (n + 1) * CELLS].astype(F32)
        z = dot(wf[...], ab_columns(wide), TN)
        total = z[ch : 2 * ch]
        total = total + shift_cells(z[0:ch], 1, 1) + shift_cells(z[2 * ch : 3 * ch], -1, 1)
        out[n] = total.astype(BF16)


def add_kernel(values, out):
    total = values[0]
    for k in range(1, values.shape[0]):
        total = total + values[k]
    for k in range(out.shape[0]):
        out[k] = total


def finish_kernel(rays, values, cw_out, cb_out, w1_out, b1_out, w2_out, loss_out):
    ch = values.shape[0]
    hid = b1_out.shape[1]
    for k in range(7):
        width = min(LANE, cw_out.shape[1] - k * LANE)
        cw_out[:, k * LANE : k * LANE + width] = values[:, k, 0:width]
    small = values[:, 7, :]
    w1_out[...] = small[:, 0:hid]
    turned = pltpu.roll(small, LANE - hid, 1)
    b1_out[...] = turned[0:1, 0:hid]
    w2_out[...] = jnp.concatenate([column(turned[1:2, 0:hid]), column(turned[2:3, 0:hid])], axis=1)
    cb_out[...] = turned[3:4, 0:ch]
    loss_out[...] = turned[4:5, 0:1] * (1.0 / rays)


VMEM = pl.BlockSpec(memory_space=pltpu.VMEM)
SMEM = pl.BlockSpec(memory_space=pltpu.SMEM)


def call(kernel, shapes, specs, args, scratch=(), name=None, flops=0, moved_bytes=0):
    shapes = [jax.ShapeDtypeStruct(s, t) for s, t in shapes]
    return pl.pallas_call(
        kernel,
        out_shape=shapes,
        in_specs=specs,
        out_specs=[VMEM] * len(shapes),
        scratch_shapes=list(scratch),
        name=name,
        cost_estimate=pl.CostEstimate(flops=flops, bytes_accessed=moved_bytes, transcendentals=0),
        compiler_params=pltpu.CompilerParams(vmem_limit_bytes=40 * 1024 * 1024),
    )(*args)


def swap(value, axis):
    return lax.all_to_all(value, axis, split_axis=0, concat_axis=0, tiled=True)


def local(
    bricks, conv_w, conv_b, head_w1, head_b1, head_w2, queries, sample_src, depth_target, inten_target, drop_label
):
    shells = lax.axis_size("shell")
    sectors = lax.axis_size("sector")
    shell = lax.axis_index("shell").astype(jnp.int32).reshape(1)
    blocks = bricks[0]
    count, ch = blocks.shape[0], blocks.shape[1]
    hid = head_w1.shape[1]
    cells = count * CELLS
    groups = cells // HI
    rays = depth_target.shape[0]
    addr = swap(queries[0], "sector")
    wf = conv_w.reshape(ch, 9, 3 * ch).transpose(1, 0, 2).reshape(9 * ch, 3 * ch)
    b1 = head_b1.reshape(1, hid)
    slots = sample_src[0].reshape(rays, SAMP).T
    dec, slope, planes, factor = call(
        decode_kernel,
        [((ch, cells), BF16), ((ch, cells), F32), ((6 * groups, HI), BF16), ((2, groups, HI), F32)],
        [VMEM] * 6,
        (blocks, wf, conv_b.reshape(1, ch), head_w1, b1, head_w2),
        scratch=[pltpu.VMEM((groups, HI), F32), pltpu.VMEM((groups, HI), F32)],
        name="decode",
        flops=2 * 10**9,
        moved_bytes=2 * 10**6,
    )
    (picked,) = call(
        owner_pick_kernel,
        [((sectors, 4, LANE), F32)],
        [VMEM] * 2,
        (addr, planes),
        name="owner_pick",
        flops=10**9,
        moved_bytes=10**5,
    )
    replies = swap(picked, "sector")
    density, intensity, terms = call(
        functools.partial(sample_kernel, shells),
        [((SAMP, rays), F32), ((SAMP, rays), F32), ((shells, 4, rays), F32)],
        [SMEM, VMEM, VMEM],
        (shell, replies, slots),
        name="sample",
        flops=10**9,
        moved_bytes=10**5,
    )
    terms = swap(terms, "shell")
    buckets, ray_depth, loss = call(
        functools.partial(render_kernel, shells),
        [((sectors, 4, LANE), F32), ((1, rays), F32), ((1, 1), F32)],
        [SMEM] + [VMEM] * 7,
        (
            shell,
            terms,
            density,
            intensity,
            slots,
            depth_target.reshape(1, rays),
            inten_target.reshape(1, rays),
            drop_label.reshape(1, rays),
        ),
        name="render",
        flops=10**9,
        moved_bytes=10**5,
    )
    cots = swap(buckets, "sector")
    payload, conv_cot = call(
        owner_back_kernel,
        [((ch, 8, LANE), F32), ((ch, cells), BF16)],
        [VMEM] * 10,
        (addr, cots, factor, dec, slope, blocks, head_w1, b1, head_w2, loss),
        scratch=[pltpu.VMEM((6, sectors, HI), F32)],
        name="owner_back",
        flops=2 * 10**9,
        moved_bytes=2 * 10**6,
    )
    share = (ch * 8 // sectors, LANE)
    part = swap(payload.reshape((sectors,) + share), "sector")
    (brick_grads,) = call(
        bricks_back_kernel,
        [(blocks.shape, BF16)],
        [VMEM] * 2,
        (conv_cot, wf),
        name="bricks_back",
        flops=2 * 10**9,
        moved_bytes=10**6,
    )
    (part,) = call(add_kernel, [((shells,) + share, F32)], [VMEM], (part,), name="add_sectors")
    part = swap(part, "shell")
    (part,) = call(add_kernel, [((sectors,) + share, F32)], [VMEM], (part,), name="add_shells")
    whole = swap(part, "sector").reshape(ch, 8, LANE)
    conv_grad, conv_b_grad, grad_one, grad_b1, grad_two, loss_mean = call(
        functools.partial(finish_kernel, rays * sectors),
        [
            (conv_w.shape, F32),
            ((1, ch), F32),
            (head_w1.shape, F32),
            ((1, hid), F32),
            (head_w2.shape, F32),
            ((1, 1), F32),
        ],
        [VMEM],
        (whole,),
        name="finish",
    )
    return (
        loss_mean.reshape(()),
        conv_grad,
        conv_b_grad.reshape(ch),
        grad_one,
        grad_b1.reshape(hid),
        grad_two,
        brick_grads[None],
        ray_depth.reshape(rays),
    )


def solution(mesh):
    return jax.shard_map(
        local,
        mesh=mesh,
        in_specs=(
            P("shell", "sector", None, None),
            P(),
            P(),
            P(),
            P(),
            P(),
            P("shell", "sector", None),
            P("shell", "sector"),
            P("sector"),
            P("sector"),
            P("sector"),
        ),
        out_specs=(P(), P(), P(), P(), P(), P(), P("shell", "sector", None, None), P("sector")),
        check_vma=False,
    )
```

time: 677 us -> 107 us (0.16); the launches traced: 665 us -> 106 us
  local copies, waits for them, and re-layouts: 249 us -> 4.42 us
  blocking collectives: 192 us -> 48 us
  other arithmetic: 70.1 us -> 0.68 us
  waiting for transfers between devices: 76.9 us -> 12.9 us
  matrix products: 25.1 us -> 0 us
  Pallas kernels: 0 us -> 20.3 us
  between operations: 16.9 us -> 0.78 us
  starting transfers between devices: 34.7 us -> 18.8 us
    psum x3 -> x0, blocking collectives: 156 us -> none  [the longest x1 72.8 us: local(): lax.psum((conv_grad, conv_bias_grad, grad_one, grad_bias_one, grad_two),...]
    unnamed x118 -> x24, local copies, waits for them, and re-layouts: 119 us -> 2.6 us
    psum x1 -> x0, waiting for transfers between devices: 65.3 us -> none  [local(): lax.psum((conv_grad, conv_bias_grad, grad_one, grad_bias_one, grad_two),...]
    reshape x31 -> x1, local copies, waits for them, and re-layouts: 58.9 us -> 0.14 us  [local(): conv_w.reshape(ch, 9, 3 * ch).transpose(1, 0, 2).reshape(9 * ch, 3 * ch)]
    all_to_all x0 -> x4, blocking collectives: none -> 48 us  [swap(): return lax.all_to_all(value, axis, split_axis=0, concat_axis=0, tiled=True)]
    scatter-add x1 -> x0, other arithmetic: 45 us -> none  [local(): table_grad = jnp.zeros((channels, brick_count * 512), jnp.float32).at[:,...]
    gather x3 -> x0, local copies, waits for them, and re-layouts: 37.1 us -> none  [the longest x2 25 us: local(): picked = jnp.take(cell_table, jnp.where(live_slot, owner_addr, 0), axis=1)]
    all_gather x2 -> x0, blocking collectives: 35.6 us -> none  [entering(): pieces = lax.all_gather(value, axis)]
  transfers between devices with their start and end apart: 4 -> 3, of which waited for: 2 -> 3; matrix products, arithmetic and copies ran while one was open for 31% -> 2% of each run, Pallas kernels for 0% -> 7%
where the time goes in v1:
time: 107 us; the launch traced here: 106 us
  blocking collectives  48 us (45%)
  Pallas kernels  20.3 us (19%)
  starting transfers between devices  18.8 us (18%)
  waiting for transfers between devices  12.9 us (12%)
  local copies, waits for them, and re-layouts  4.42 us (4%)
    all_to_all x4, blocking collectives, swap(): return lax.all_to_all(value, axis, split_axis=0, concat_axis=0, tiled=True)  48 us
    pallas_call x9, Pallas kernels, call(): pl.pallas_call(kernel, out_shape=shapes, in_specs=specs, out_specs=[VMEM]...  20.3 us
    all_to_all x3, starting transfers between devices, swap(): return lax.all_to_all(value, axis, split_axis=0, concat_axis=0, tiled=True)  18.8 us
    all_to_all x3, waiting for transfers between devices, swap(): return lax.all_to_all(value, axis, split_axis=0, concat_axis=0, tiled=True)  12.9 us
    unnamed x24, local copies, waits for them, and re-layouts  2.6 us
  transfers between devices with their start and end apart: 3, of which 3 were waited for; matrix products, arithmetic and copies ran while one was open for 2% of the time, Pallas kernels for 7%

profile of v1, /device:TPU:1, one launch (start us, length us, event | category | flops | bytes accessed | tf_op | source)
XLA Modules:
  0.0 105.9 jit_solution(15623992231042840279)
XLA Ops:
  0.6 0.0 copy-start.9
  0.6 0.0 copy-start.7
  0.7 1.4 %all_to_all.25 = s32[32,1,256]{2,1,0:T(1,128)} reshape(s32[1,32,256]{2,1,0:T(8,128)} %param.17) | data formatting | bytes 65536 | tf_op jit(solution)/shard_map/all_to_all | solution.py:393
  2.1 0.0 copy-start
  2.1 8.7 %all-to-all-start = ((s32[32,1,256]{2,1,0:T(1,128)}), s32[32,1,256]{2,1,0:T(1,128)S(1)}, u32[]{:S(2)}, u32[]{:S(2)}) async-start(s32[32,1,256]{2,1,0:T(1,128)} %all_to_all.25), calls=%async_computation | async-start | bytes 65536 | tf_op jit(solution)/shard_map/all_to_all | solution.py:393
  10.8 0.0 copy-done.9
  10.8 0.1 copy.29.w2
  10.9 0.0 copy-done.7
  10.9 0.1 reshape.56
  11.1 0.0 copy-start.1
  11.1 0.0 copy-start.5
  11.1 0.0 copy-start.6
  11.1 0.0 copy-done
  11.1 0.6 copy-done.1
  11.8 0.0 copy-done.5
  11.8 0.0 copy-done.6
  11.8 3.8 %decode.1 = (bf16[32,4096]{1,0:T(8,128)(2,1)S(1)}, f32[32,4096]{1,0:T(8,128)S(1)}, bf16[96,256]{1,0:T(8,128)(2,1)S(1)}, f32[2,16,256]{2,1,0:T(8,128)S(1)}) custom-call(bf16[8,32,512]{2,1,0:T(8,128)(2,1)S(1)} %bitcast.24, bf16[288,96]{1,0:T(8,128)(2,1)S(1)} %bitcast.18, f32[1,32]{1,0:T(1,128)S(1)} %bitcast.29, bf16[32,64]{1,0:T(8,128)(2,1)S(1)} %copy-done.1, ...), custom_call_target="tpu_custom_call" | custom-call | flops 2000000000 | bytes 2000000 | tf_op jit(solution)/shard_map/decode/pallas_call | solution.py:380
  15.6 2.5 %all-to-all-done = s32[32,1,256]{2,1,0:T(1,128)S(1)} async-done(((s32[32,1,256]{2,1,0:T(1,128)}), s32[32,1,256]{2,1,0:T(1,128)S(1)}, u32[]{:S(2)}, u32[]{:S(2)}) %all-to-all-start) | async-done | bytes 32800 | tf_op jit(solution)/shard_map/all_to_all | solution.py:393
  18.1 2.6 %owner_pick.1 = f32[32,4,128]{2,1,0:T(4,128)} custom-call(s32[32,256]{1,0:T(8,128)S(1)} %bitcast.20, bf16[96,256]{1,0:T(8,128)(2,1)S(1)} %get-tuple-element.26.planes), custom_call_target="tpu_custom_call" | custom-call | flops 1000000000 | bytes 100000 | tf_op jit(solution)/shard_map/owner_pick/pallas_call | solution.py:380
  20.6 0.0 copy-start.8
  20.6 5.0 %all-to-all-start.1 = ((f32[32,4,128]{2,1,0:T(4,128)}), f32[32,4,128]{2,1,0:T(4,128)S(1)}, u32[]{:S(2)}, u32[]{:S(2)}) async-start(f32[32,4,128]{2,1,0:T(4,128)} %owner_pick.1), calls=%async_computation.1 | async-start | bytes 131072 | tf_op jit(solution)/shard_map/all_to_all | solution.py:393
  25.7 0.5 broadcast.3
  26.2 0.0 copy-done.8
  26.2 0.7 reduce.3
  26.9 0.2 reshape_squeeze.3
  27.1 0.1 copy.30
  27.2 5.9 %all-to-all-done.1.replies = f32[32,4,128]{2,1,0:T(4,128)S(1)} async-done(((f32[32,4,128]{2,1,0:T(4,128)}), f32[32,4,128]{2,1,0:T(4,128)S(1)}, u32[]{:S(2)}, u32[]{:S(2)}) %all-to-all-start.1) | async-done | bytes 65568 | tf_op jit(solution)/shard_map/all_to_all | solution.py:393
  33.1 0.0 copy-start.3
  33.1 0.0 copy-start.4
  33.1 0.9 sample.1
  34.0 15.2 %all_to_all.41.terms = f32[8,4,512]{2,1,0:T(4,128)S(1)} all-to-all(f32[8,4,512]{2,1,0:T(4,128)S(1)} %get-tuple-element.27), channel_id=1, replica_groups=mesh['shell'=8,'sector'=32] {'shell'}, dimensions={0} | all-to-all | bytes 131072 | tf_op jit(solution)/shard_map/all_to_all | solution.py:393
  49.2 0.0 copy-start.2
  49.2 0.0 copy-done.3
  49.2 0.0 copy-done.4
  49.2 0.7 copy-done.2
  49.9 1.3 %render.1 = (f32[32,4,128]{2,1,0:T(4,128)S(1)}, f32[1,512]{1,0:T(1,128)}, f32[1,1]{1,0:T(1,128)}) custom-call(s32[1]{0:T(128)} %bitcast.shell_ref, f32[8,4,512]{2,1,0:T(4,128)S(1)} %all_to_all.41.terms, f32[8,512]{1,0:T(8,128)S(1)} %get-tuple-element.28.density, f32[8,512]{1,0:T(8,128)S(1)} %get-tuple-element.29.intensity, s32[8,512]{1,0:T(8,128)S(1)} %bitcast.23, ...), custom_call_target="tpu_custom_call" | custom-call | flops 1000000000 | bytes 100000 | tf_op jit(solution)/shard_map/render/pallas_call | solution.py:380
  51.2 12.3 %all_to_all.42.cots = f32[32,4,128]{2,1,0:T(4,128)S(1)} all-to-all(f32[32,4,128]{2,1,0:T(4,128)S(1)} %get-tuple-element.30), channel_id=1, replica_groups=mesh['shell'=8,'sector'=32] {'sector'}, dimensions={0} | all-to-all | bytes 131072 | tf_op jit(solution)/shard_map/all_to_all | solution.py:393
  63.5 6.9 %owner_back.1 = (f32[32,8,128]{2,1,0:T(8,128)S(1)}, bf16[32,4096]{1,0:T(8,128)(2,1)S(1)}) custom-call(s32[32,256]{1,0:T(8,128)S(1)} %bitcast.21, f32[32,4,128]{2,1,0:T(4,128)S(1)} %all_to_all.42.cots, f32[2,16,256]{2,1,0:T(8,128)S(1)} %get-tuple-element.31.factor, bf16[32,4096]{1,0:T(8,128)(2,1)S(1)} %get-tuple-element.32.dec, ...), custom_call_target="tpu_custom_call" | custom-call | flops 2000000000 | bytes 2000000 | tf_op jit(solution)/shard_map/owner_back/pallas_call | solution.py:380
  70.4 11.2 %all_to_all.43.values = f32[32,8,128]{2,1,0:T(8,128)S(1)} all-to-all(f32[32,8,128]{2,1,0:T(8,128)S(1)} %get-tuple-element.35), channel_id=1, replica_groups=mesh['shell'=8,'sector'=32] {'sector'}, dimensions={0} | all-to-all | bytes 262144 | tf_op jit(solution)/shard_map/all_to_all | solution.py:393
  81.7 9.2 %all_to_all.44.values = f32[8,8,128]{2,1,0:T(8,128)S(1)} all-to-all(f32[8,8,128]{2,1,0:T(8,128)S(1)} %add_sectors.1), channel_id=1, replica_groups=mesh['shell'=8,'sector'=32] {'shell'}, dimensions={0} | all-to-all | bytes 65536 | tf_op jit(solution)/shard_map/all_to_all | solution.py:393
  90.9 0.7 add_shells.1
  91.6 5.0 %all-to-all-start.6 = ((f32[32,8,128]{2,1,0:T(8,128)}), f32[32,8,128]{2,1,0:T(8,128)S(1)}, u32[]{:S(2)}, u32[]{:S(2)}) async-start(f32[32,8,128]{2,1,0:T(8,128)} %add_shells.1), calls=%async_computation.6 | async-start | bytes 262144 | tf_op jit(solution)/shard_map/all_to_all | solution.py:393
  96.6 3.3 %bricks_back.1 = bf16[8,32,512]{2,1,0:T(8,128)(2,1)} custom-call(bf16[32,4096]{1,0:T(8,128)(2,1)S(1)} %get-tuple-element.42.cot, bf16[288,96]{1,0:T(8,128)(2,1)S(1)} %bitcast.19), custom_call_target="tpu_custom_call" | custom-call | flops 2000000000 | bytes 1000000 | tf_op jit(solution)/shard_map/bricks_back/pallas_call | solution.py:380
  99.9 4.6 %all-to-all-done.6.values = f32[32,8,128]{2,1,0:T(8,128)S(1)} async-done(((f32[32,8,128]{2,1,0:T(8,128)}), f32[32,8,128]{2,1,0:T(8,128)S(1)}, u32[]{:S(2)}, u32[]{:S(2)}) %all-to-all-start.6) | async-done | bytes 131104 | tf_op jit(solution)/shard_map/all_to_all | solution.py:393
  104.5 0.8 finish.1
  105.3 0.6 copy.32
  (3 shorter events, 0.1 us)
Async XLA Ops:
  0.6 10.2 %copy-start.9 = (f32[64,2]{0,1:T(2,128)S(1)}, f32[64,2]{0,1:T(2,128)}, u32[]{:S(2)}) copy-start(f32[64,2]{0,1:T(2,128)} %param.16) | copy-start | bytes 1540
  0.6 10.3 %copy-start.7 = (bf16[32,864]{1,0:T(8,128)(2,1)S(1)}, bf16[32,864]{1,0:T(8,128)(2,1)}, u32[]{:S(2)}) copy-start(bf16[32,864]{1,0:T(8,128)(2,1)} %param.12) | copy-start | bytes 165892
  2.1 9.0 %copy-start = (bf16[1,8,32,512]{3,2,1,0:T(8,128)(2,1)S(1)}, bf16[1,8,32,512]{3,2,1,0:T(8,128)(2,1)}, u32[]{:S(2)}) copy-start(bf16[1,8,32,512]{3,2,1,0:T(8,128)(2,1)} %param.11) | copy-start | bytes 786436
  2.1 16.0 %all-to-all-start = ((s32[32,1,256]{2,1,0:T(1,128)}), s32[32,1,256]{2,1,0:T(1,128)S(1)}, u32[]{:S(2)}, u32[]{:S(2)}) async-start(s32[32,1,256]{2,1,0:T(1,128)} %all_to_all.25), calls=%async_computation | async-start | bytes 65536 | tf_op jit(solution)/shard_map/all_to_all | solution.py:393
  11.1 0.7 copy-start.1
  11.1 0.7 copy-start.5
  11.1 0.7 copy-start.6
  20.6 5.6 %copy-start.8 = (s32[1,4096]{1,0:T(1,128)S(1)}, s32[1,4096]{1,0:T(1,128)}, u32[]{:S(2)}) copy-start(s32[1,4096]{1,0:T(1,128)} %param.18) | copy-start | bytes 49156
  20.6 12.4 %all-to-all-start.1 = ((f32[32,4,128]{2,1,0:T(4,128)}), f32[32,4,128]{2,1,0:T(4,128)S(1)}, u32[]{:S(2)}, u32[]{:S(2)}) async-start(f32[32,4,128]{2,1,0:T(4,128)} %owner_pick.1), calls=%async_computation.1 | async-start | bytes 131072 | tf_op jit(solution)/shard_map/all_to_all | solution.py:393
  33.1 16.2 %copy-start.3 = (f32[512]{0:T(512)S(1)}, f32[512]{0:T(512)}, u32[]{:S(2)}) copy-start(f32[512]{0:T(512)} %param.20) | copy-start | bytes 6148
  33.1 16.2 %copy-start.4 = (s32[512]{0:T(512)S(1)}, s32[512]{0:T(512)}, u32[]{:S(2)}) copy-start(s32[512]{0:T(512)} %param.21) | copy-start | bytes 6148
  49.2 0.7 copy-start.2
  91.6 12.9 %all-to-all-start.6 = ((f32[32,8,128]{2,1,0:T(8,128)}), f32[32,8,128]{2,1,0:T(8,128)S(1)}, u32[]{:S(2)}, u32[]{:S(2)}) async-start(f32[32,8,128]{2,1,0:T(8,128)} %add_shells.1), calls=%async_computation.6 | async-start | bytes 262144 | tf_op jit(solution)/shard_map/all_to_all | solution.py:393

commit v2 on v1

--- a/solution.py
+++ b/solution.py
@@ -88,12 +88,33 @@
     return jnp.concatenate(parts, axis=0).astype(BF16)
 
 
-def decode_kernel(bricks, wf, conv_b, w1, b1, w2, dec_out, slope_out, planes_out, factor_out, e0_s, e1_s):
+def offset_rows(conv_w):
+    ch = conv_w.shape[0]
+    width = 3 * ch
+    wide = conv_w[...].astype(F32)
+    tiles = [wide[:, k * LANE : (k + 1) * LANE] for k in range(wide.shape[1] // LANE)]
+    lane = iota((ch, LANE), 1)
+    rows = []
+    for ab in range(9):
+        tile, off = divmod(width * ab, LANE)
+        if off == 0:
+            rows.append(wide[:, tile * LANE : tile * LANE + width])
+            continue
+        block = pltpu.roll(tiles[tile], LANE - off, 1)
+        if off + width > LANE:
+            block = jnp.where(lane < LANE - off, block, pltpu.roll(tiles[tile + 1], LANE - off, 1))
+        rows.append(block[:, 0:width])
+    return jnp.concatenate(rows, axis=0).astype(BF16)
+
+
+def decode_kernel(bricks, conv_w, conv_b, w1, b1, w2t, dec_out, slope_out, planes_out, factor_out, e0_s, e1_s):
     count, ch = bricks.shape[0], bricks.shape[1]
     bias = column(conv_b[...])
     bias1 = column(b1[...])
+    w2_0, w2_1 = column(w2t[0:1, :]), column(w2t[1:2, :])
+    wf = offset_rows(conv_w)
     for n in range(count):
-        y = dot(wf[...], c_columns(bricks[n]))
+        y = dot(wf, c_columns(bricks[n]))
         pre = bias
         for a in range(3):
             rows = [y[(3 * a + b) * ch : (3 * a + b + 1) * ch] for b in range(3)]
@@ -103,10 +124,9 @@
         dec = value.astype(BF16)
         dec_out[:, n * CELLS : (n + 1) * CELLS] = dec
         slope_out[:, n * CELLS : (n + 1) * CELLS] = slope
-        h = dot(w1[...], dec, TN) + bias1
-        g, _ = gelu_pair(h)
-        e0 = jnp.sum(w2[:, 0:1] * g, axis=0, keepdims=True)
-        e1 = jnp.sum(w2[:, 1:2] * g, axis=0, keepdims=True)
+        g = gelu_pair(dot(w1[...], dec, TN) + bias1)[0]
+        e0 = jnp.sum(w2_0 * g, axis=0, keepdims=True)
+        e1 = jnp.sum(w2_1 * g, axis=0, keepdims=True)
         for half in range(CELLS // HI):
             at = n * (CELLS // HI) + half
             e0_s[at : at + 1, :] = e0[:, half * HI : (half + 1) * HI]
@@ -120,6 +140,29 @@
     planes_out[...] = jnp.concatenate(split3(density) + split3(intensity), axis=0).astype(BF16)
 
 
+def rays_last(sources):
+    width = SAMP * LANE // 2
+    rays = sources.shape[1] // SAMP
+    lane = iota((SAMP, width), 1)
+    mine = (lane & (SAMP - 1)) == iota((SAMP, width), 0)
+    chosen = (iota((width, LANE // 2), 0) >> 3) == iota((width, LANE // 2), 1)
+    chosen = jnp.where(chosen, 1.0, 0.0).astype(BF16)
+    blocks = [jnp.where(mine, sources[:, k * width : (k + 1) * width], 0) for k in range(2 * rays // LANE)]
+    stack = jnp.concatenate(blocks, axis=0)
+    high = dot((stack >> 8).astype(F32).astype(BF16), chosen)
+    low = dot((stack & 255).astype(F32).astype(BF16), chosen)
+    whole = (high * 256.0 + low).astype(jnp.int32)
+    parts = [whole[k * SAMP : (k + 1) * SAMP] for k in range(2 * rays // LANE)]
+    return jnp.concatenate(parts, axis=1)
+
+
+def arrange_kernel(target, inten_target, drop, sources, targets_out, slots_out):
+    targets_out[0:1, :] = target[...]
+    targets_out[1:2, :] = inten_target[...]
+    targets_out[2:3, :] = drop[...].astype(F32)
+    slots_out[...] = rays_last(sources)
+
+
 def one_hot(low):
     return jnp.where(iota((HI, low.shape[1]), 0) == low, 1.0, 0.0).astype(BF16)
 
@@ -150,15 +193,11 @@
 
 def owner_pick_kernel(addr, planes, out):
     groups = planes.shape[0] // 6
-
-    def body(s, carry):
-        pair = pick(planes[...], groups, addr[pl.ds(s, 1), :])
+    for s in range(addr.shape[0]):
+        pair = pick(planes[...], groups, addr[s])
         for v in range(2):
             for half in range(2):
                 out[s, 2 * v + half : 2 * v + half + 1, :] = pair[v][:, half * LANE : (half + 1) * LANE]
-        return carry
-
-    lax.fori_loop(0, addr.shape[0], body, 0, unroll=4)
 
 
 def excl_down(x):
@@ -210,7 +249,7 @@
 
 
 def render_kernel(
-    shells, shell_ref, terms, density, intensity, slots, target, inten_target, drop, buckets_out, depth_out, loss_out
+    shells, shell_ref, terms, density, intensity, slots, targets, buckets_out, depth_out, loss_out
 ):
     shell = shell_ref[0]
     delta = 2.0 / (shells * SAMP)
@@ -221,10 +260,10 @@
     ray_depth = jnp.sum(entry * d_all, axis=0, keepdims=True)
     ray_inten = jnp.sum(entry * i_all, axis=0, keepdims=True)
     escape = jnp.exp(-jnp.sum(t_all, axis=0, keepdims=True))
-    dropped = drop[...].astype(F32)
+    dropped = targets[2:3, :]
     kept = 1.0 - dropped
-    depth_err = ray_depth - target[...]
-    inten_err = ray_inten - inten_target[...]
+    depth_err = ray_depth - targets[0:1, :]
+    inten_err = ray_inten - targets[1:2, :]
     loss = kept * (depth_err * depth_err + inten_err * inten_err) + (escape - dropped) * (escape - dropped)
     loss_out[...] = jnp.where(shell == 0, jnp.sum(loss, axis=1, keepdims=True), 0.0)
     depth_out[...] = ray_depth
@@ -263,7 +302,7 @@
 
 
 def owner_back_kernel(
-    addr, cots, factor, dec, slope, bricks, w1, b1, w2, loss, payload_out, cot_out, plane_s
+    addr, cots, factor, dec, slope, bricks, w1, b1, w2t, loss, payload_out, cot_out, plane_s
 ):
     count, ch = bricks.shape[0], bricks.shape[1]
     hid = w1.shape[1]
@@ -275,14 +314,13 @@
             plane_s[3 * v + k] = part
 
     def body(s, acc):
-        rows = [plane_s[k, pl.ds(s, 1), :] for k in range(6)]
-        return acc + spread(rows, groups, addr[pl.ds(s, 1), :])
-
-    acc = lax.fori_loop(0, sectors, body, jnp.zeros((6 * groups, HI), F32), unroll=4)
+        return acc + spread([plane_s[k, pl.ds(s, 1), :] for k in range(6)], groups, addr[s])
+
+    acc = lax.fori_loop(0, sectors, body, jnp.zeros((6 * groups, HI), F32), unroll=16)
     pair = join_planes(acc, groups)
     ge = [pair[v] * factor[v] for v in range(2)]
     bias1 = column(b1[...])
-    w2_0, w2_1 = w2[:, 0:1], w2[:, 1:2]
+    w2_0, w2_1 = column(w2t[0:1, :]), column(w2t[1:2, :])
     per = CELLS // HI
     acc_w1 = jnp.zeros((ch, hid), F32)
     acc_b1 = jnp.zeros((hid, LANE), F32)
@@ -338,11 +376,12 @@
     payload_out[:, 7, :] = jnp.concatenate([acc_w1, jnp.concatenate(small, axis=0)], axis=1)
 
 
-def bricks_back_kernel(cot, wf, out):
+def bricks_back_kernel(cot, conv_w, out):
     count, ch = out.shape[0], out.shape[1]
+    wf = offset_rows(conv_w)
     for n in range(count):
         wide = cot[:, n * CELLS : (n + 1) * CELLS].astype(F32)
-        z = dot(wf[...], ab_columns(wide), TN)
+        z = dot(wf, ab_columns(wide), TN)
         total = z[ch : 2 * ch]
         total = total + shift_cells(z[0:ch], 1, 1) + shift_cells(z[2 * ch : 3 * ch], -1, 1)
         out[n] = total.astype(BF16)
@@ -366,7 +405,7 @@
     w1_out[...] = small[:, 0:hid]
     turned = pltpu.roll(small, LANE - hid, 1)
     b1_out[...] = turned[0:1, 0:hid]
-    w2_out[...] = jnp.concatenate([column(turned[1:2, 0:hid]), column(turned[2:3, 0:hid])], axis=1)
+    w2_out[...] = turned[1:3, 0:hid]
     cb_out[...] = turned[3:4, 0:ch]
     loss_out[...] = turned[4:5, 0:1] * (1.0 / rays)
 
@@ -375,17 +414,17 @@
 SMEM = pl.BlockSpec(memory_space=pltpu.SMEM)
 
 
-def call(kernel, shapes, specs, args, scratch=(), name=None, flops=0, moved_bytes=0):
+def call(kernel, shapes, specs, args, scratch=(), name=None, flops=0, moved_bytes=0, out_specs=None):
     shapes = [jax.ShapeDtypeStruct(s, t) for s, t in shapes]
     return pl.pallas_call(
         kernel,
         out_shape=shapes,
         in_specs=specs,
-        out_specs=[VMEM] * len(shapes),
+        out_specs=out_specs or [VMEM] * len(shapes),
         scratch_shapes=list(scratch),
         name=name,
         cost_estimate=pl.CostEstimate(flops=flops, bytes_accessed=moved_bytes, transcendentals=0),
-        compiler_params=pltpu.CompilerParams(vmem_limit_bytes=40 * 1024 * 1024),
+        compiler_params=pltpu.CompilerParams(vmem_limit_bytes=16 * 1024 * 1024),
     )(*args)
 
 
@@ -405,15 +444,14 @@
     cells = count * CELLS
     groups = cells // HI
     rays = depth_target.shape[0]
-    addr = swap(queries[0], "sector")
-    wf = conv_w.reshape(ch, 9, 3 * ch).transpose(1, 0, 2).reshape(9 * ch, 3 * ch)
+    addr = swap(queries[0].reshape(sectors, 1, HI), "sector")
     b1 = head_b1.reshape(1, hid)
-    slots = sample_src[0].reshape(rays, SAMP).T
+    w2t = head_w2.T
     dec, slope, planes, factor = call(
         decode_kernel,
         [((ch, cells), BF16), ((ch, cells), F32), ((6 * groups, HI), BF16), ((2, groups, HI), F32)],
         [VMEM] * 6,
-        (blocks, wf, conv_b.reshape(1, ch), head_w1, b1, head_w2),
+        (blocks, conv_w, conv_b.reshape(1, ch), head_w1, b1, w2t),
         scratch=[pltpu.VMEM((groups, HI), F32), pltpu.VMEM((groups, HI), F32)],
         name="decode",
         flops=2 * 10**9,
@@ -425,6 +463,20 @@
         [VMEM] * 2,
         (addr, planes),
         name="owner_pick",
+        flops=10**9,
+        moved_bytes=10**5,
+    )
+    targets, slots = call(
+        arrange_kernel,
+        [((3, rays), F32), ((SAMP, rays), jnp.int32)],
+        [VMEM] * 4,
+        (
+            depth_target.reshape(1, rays),
+            inten_target.reshape(1, rays),
+            drop_label.reshape(1, rays),
+            lax.optimization_barrier((sample_src, picked))[0],
+        ),
+        name="arrange",
         flops=10**9,
         moved_bytes=10**5,
     )
@@ -442,17 +494,8 @@
     buckets, ray_depth, loss = call(
         functools.partial(render_kernel, shells),
         [((sectors, 4, LANE), F32), ((1, rays), F32), ((1, 1), F32)],
-        [SMEM] + [VMEM] * 7,
-        (
-            shell,
-            terms,
-            density,
-            intensity,
-            slots,
-            depth_target.reshape(1, rays),
-            inten_target.reshape(1, rays),
-            drop_label.reshape(1, rays),
-        ),
+        [SMEM] + [VMEM] * 5,
+        (shell, terms, density, intensity, slots, targets),
         name="render",
         flops=10**9,
         moved_bytes=10**5,
@@ -462,7 +505,7 @@
         owner_back_kernel,
         [((ch, 8, LANE), F32), ((ch, cells), BF16)],
         [VMEM] * 10,
-        (addr, cots, factor, dec, slope, blocks, head_w1, b1, head_w2, loss),
+        (addr, cots, factor, dec, slope, blocks, head_w1, b1, w2t, loss),
         scratch=[pltpu.VMEM((6, sectors, HI), F32)],
         name="owner_back",
         flops=2 * 10**9,
@@ -474,7 +517,7 @@
         bricks_back_kernel,
         [(blocks.shape, BF16)],
         [VMEM] * 2,
-        (conv_cot, wf),
+        (conv_cot, conv_w),
         name="bricks_back",
         flops=2 * 10**9,
         moved_bytes=10**6,
@@ -490,7 +533,7 @@
             ((1, ch), F32),
             (head_w1.shape, F32),
             ((1, hid), F32),
-            (head_w2.shape, F32),
+            (w2t.shape, F32),
             ((1, 1), F32),
         ],
         [VMEM],
@@ -503,7 +546,7 @@
         conv_b_grad.reshape(ch),
         grad_one,
         grad_b1.reshape(hid),
-        grad_two,
+        grad_two.T,
         brick_grads[None],
         ray_depth.reshape(rays),
     )

time: 107 us -> 104 us (0.972)
  Pallas kernels: 20.3 us -> 17.9 us
    pallas_call x9 -> x10, Pallas kernels: 20.3 us -> 17.9 us  [call(): pl.pallas_call(kernel, out_shape=shapes, in_specs=specs, out_specs=out_sp...]
    all_to_all x1 -> x0, local copies, waits for them, and re-layouts: 1.42 us -> none  [swap(): return lax.all_to_all(value, axis, split_axis=0, concat_axis=0, tiled=True)]
    another operation x2 -> x1, local copies, waits for them, and re-layouts: 0.25 us -> 1.41 us  [local(): addr = swap(queries[0].reshape(sectors, 1, HI), 'sector')]
    unnamed x24 -> x22, local copies, waits for them, and re-layouts: 2.6 us -> 2.28 us
  transfers between devices with their start and end apart: 3 -> 3, of which waited for: 3 -> 3; matrix products, arithmetic and copies ran while one was open for 2% -> 0% of each run, Pallas kernels for 7% -> 7%
where the time goes in v2:
time: 104 us; the launch traced here: 103 us
  blocking collectives  48 us (46%)
  starting transfers between devices  19.8 us (19%)
  Pallas kernels  17.9 us (17%)
  waiting for transfers between devices  13.2 us (13%)
  local copies, waits for them, and re-layouts  3.69 us (4%)
    all_to_all x4, blocking collectives, swap(): return lax.all_to_all(value, axis, split_axis=0, concat_axis=0, tiled=True)  48 us
    all_to_all x3, starting transfers between devices, swap(): return lax.all_to_all(value, axis, split_axis=0, concat_axis=0, tiled=True)  19.8 us
    pallas_call x10, Pallas kernels, call(): pl.pallas_call(kernel, out_shape=shapes, in_specs=specs, out_specs=out_sp...  17.9 us
    all_to_all x3, waiting for transfers between devices, swap(): return lax.all_to_all(value, axis, split_axis=0, concat_axis=0, tiled=True)  13.2 us
    unnamed x22, local copies, waits for them, and re-layouts  2.28 us
  transfers between devices with their start and end apart: 3, of which 3 were waited for; matrix products, arithmetic and copies ran while one was open for 0% of the time, Pallas kernels for 7%

profile of v2, /device:TPU:1, one launch (start us, length us, event | category | flops | bytes accessed | tf_op | source)
XLA Modules:
  0.0 103.4 jit_solution(5689847606194594021)
XLA Ops:
  0.6 0.0 copy-start.2
  0.6 1.4 %reshape_squeeze.3 = s32[32,1,256]{2,1,0:T(1,128)} reshape(s32[1,32,256]{2,1,0:T(8,128)} %param.17) | data formatting | bytes 65536 | tf_op jit(solution)/shard_map/reshape;squeeze | solution.py:447
  2.1 0.0 copy-start.4
  2.1 8.7 %all-to-all-start = ((s32[32,1,256]{2,1,0:T(1,128)}), s32[32,1,256]{2,1,0:T(1,128)S(1)}, u32[]{:S(2)}, u32[]{:S(2)}) async-start(s32[32,1,256]{2,1,0:T(1,128)} %reshape_squeeze.3), calls=%async_computation | async-start | bytes 65536 | tf_op jit(solution)/shard_map/all_to_all | solution.py:432
  10.8 0.0 copy-start.10
  10.8 0.0 copy-start.8
  10.8 0.0 copy-start.9
  10.8 0.0 copy-done.2
  10.8 0.0 copy-done.4
  10.8 0.6 copy-done.10
  11.4 0.0 copy-done.8
  11.5 0.0 copy-done.9
  11.5 0.0 copy-start
  11.5 0.9 copy-done
  12.4 4.1 %decode.1 = (bf16[32,4096]{1,0:T(8,128)(2,1)S(1)}, f32[32,4096]{1,0:T(8,128)S(1)}, bf16[96,256]{1,0:T(8,128)(2,1)S(1)}, f32[2,16,256]{2,1,0:T(8,128)S(1)}) custom-call(bf16[8,32,512]{2,1,0:T(8,128)(2,1)S(1)} %bitcast.14, bf16[32,864]{1,0:T(8,128)(2,1)S(1)} %copy-done.2, f32[1,32]{1,0:T(1,128)S(1)} %bitcast.21, bf16[32,64]{1,0:T(8,128)(2,1)S(1)} %copy-done.4, ...), custom_call_target="tpu_custom_call" | custom-call | flops 2000000000 | bytes 2000000 | tf_op jit(solution)/shard_map/decode/pallas_call | solution.py:419
  16.6 1.5 %all-to-all-done.addr = s32[32,1,256]{2,1,0:T(1,128)S(1)} async-done(((s32[32,1,256]{2,1,0:T(1,128)}), s32[32,1,256]{2,1,0:T(1,128)S(1)}, u32[]{:S(2)}, u32[]{:S(2)}) %all-to-all-start) | async-done | bytes 32800 | tf_op jit(solution)/shard_map/all_to_all | solution.py:432
  18.1 1.6 %owner_pick.1 = f32[32,4,128]{2,1,0:T(4,128)} custom-call(s32[32,1,256]{2,1,0:T(1,128)S(1)} %all-to-all-done.addr, bf16[96,256]{1,0:T(8,128)(2,1)S(1)} %get-tuple-element.29.planes), custom_call_target="tpu_custom_call" | custom-call | flops 1000000000 | bytes 100000 | tf_op jit(solution)/shard_map/owner_pick/pallas_call | solution.py:419
  19.7 0.0 copy-start.3
  19.7 0.0 copy-start.6
  19.7 0.0 copy-start.7
  19.7 6.0 %all-to-all-start.1 = ((f32[32,4,128]{2,1,0:T(4,128)}), f32[32,4,128]{2,1,0:T(4,128)S(1)}, u32[]{:S(2)}, u32[]{:S(2)}) async-start(f32[32,4,128]{2,1,0:T(4,128)} %owner_pick.1), calls=%async_computation.1 | async-start | bytes 131072 | tf_op jit(solution)/shard_map/all_to_all | solution.py:432
  25.7 0.0 copy-start.5
  25.7 0.0 copy-done.3
  25.7 0.0 copy-done.6
  25.7 0.0 copy-done.7
  25.7 0.6 copy-done.5
  26.4 0.3 arrange.1
  26.7 6.4 %all-to-all-done.1.replies = f32[32,4,128]{2,1,0:T(4,128)S(1)} async-done(((f32[32,4,128]{2,1,0:T(4,128)}), f32[32,4,128]{2,1,0:T(4,128)S(1)}, u32[]{:S(2)}, u32[]{:S(2)}) %all-to-all-start.1) | async-done | bytes 65568 | tf_op jit(solution)/shard_map/all_to_all | solution.py:432
  33.1 0.9 sample.1
  34.0 15.2 %all_to_all.35.terms = f32[8,4,512]{2,1,0:T(4,128)S(1)} all-to-all(f32[8,4,512]{2,1,0:T(4,128)S(1)} %get-tuple-element.32), channel_id=1, replica_groups=mesh['shell'=8,'sector'=32] {'shell'}, dimensions={0} | all-to-all | bytes 131072 | tf_op jit(solution)/shard_map/all_to_all | solution.py:432
  49.2 0.0 copy-start.1
  49.2 1.3 %render.1 = (f32[32,4,128]{2,1,0:T(4,128)S(1)}, f32[1,512]{1,0:T(1,128)}, f32[1,1]{1,0:T(1,128)}) custom-call(s32[1]{0:T(128)} %bitcast.shell_ref, f32[8,4,512]{2,1,0:T(4,128)S(1)} %all_to_all.35.terms, f32[8,512]{1,0:T(8,128)S(1)} %get-tuple-element.33.density, f32[8,512]{1,0:T(8,128)S(1)} %get-tuple-element.34.intensity, ...), custom_call_target="tpu_custom_call" | custom-call | flops 1000000000 | bytes 100000 | tf_op jit(solution)/shard_map/render/pallas_call | solution.py:419
  50.5 12.3 %all_to_all.36.cots = f32[32,4,128]{2,1,0:T(4,128)S(1)} all-to-all(f32[32,4,128]{2,1,0:T(4,128)S(1)} %get-tuple-element.36), channel_id=1, replica_groups=mesh['shell'=8,'sector'=32] {'sector'}, dimensions={0} | all-to-all | bytes 131072 | tf_op jit(solution)/shard_map/all_to_all | solution.py:432
  62.8 0.0 copy-done.1
  62.8 5.8 %owner_back.1 = (f32[32,8,128]{2,1,0:T(8,128)S(1)}, bf16[32,4096]{1,0:T(8,128)(2,1)S(1)}) custom-call(s32[32,1,256]{2,1,0:T(1,128)S(1)} %all-to-all-done.addr, f32[32,4,128]{2,1,0:T(4,128)S(1)} %all_to_all.36.cots, f32[2,16,256]{2,1,0:T(8,128)S(1)} %get-tuple-element.37.factor, bf16[32,4096]{1,0:T(8,128)(2,1)S(1)} %get-tuple-element.38.dec, ...), custom_call_target="tpu_custom_call" | custom-call | flops 2000000000 | bytes 2000000 | tf_op jit(solution)/shard_map/owner_back/pallas_call | solution.py:419
  68.6 11.2 %all_to_all.37.values = f32[32,8,128]{2,1,0:T(8,128)S(1)} all-to-all(f32[32,8,128]{2,1,0:T(8,128)S(1)} %get-tuple-element.41), channel_id=1, replica_groups=mesh['shell'=8,'sector'=32] {'sector'}, dimensions={0} | all-to-all | bytes 262144 | tf_op jit(solution)/shard_map/all_to_all | solution.py:432
  79.8 9.2 %all_to_all.38.values = f32[8,8,128]{2,1,0:T(8,128)S(1)} all-to-all(f32[8,8,128]{2,1,0:T(8,128)S(1)} %add_sectors.1), channel_id=1, replica_groups=mesh['shell'=8,'sector'=32] {'shell'}, dimensions={0} | all-to-all | bytes 65536 | tf_op jit(solution)/shard_map/all_to_all | solution.py:432
  89.1 0.7 add_shells.1
  89.7 5.0 %all-to-all-start.6 = ((f32[32,8,128]{2,1,0:T(8,128)}), f32[32,8,128]{2,1,0:T(8,128)S(1)}, u32[]{:S(2)}, u32[]{:S(2)}) async-start(f32[32,8,128]{2,1,0:T(8,128)} %add_shells.1), calls=%async_computation.6 | async-start | bytes 262144 | tf_op jit(solution)/shard_map/all_to_all | solution.py:432
  94.8 2.5 %bricks_back.1 = bf16[8,32,512]{2,1,0:T(8,128)(2,1)} custom-call(bf16[32,4096]{1,0:T(8,128)(2,1)S(1)} %get-tuple-element.48.cot, bf16[32,864]{1,0:T(8,128)(2,1)S(1)} %copy-done.2), custom_call_target="tpu_custom_call" | custom-call | flops 2000000000 | bytes 1000000 | tf_op jit(solution)/shard_map/bricks_back/pallas_call | solution.py:419
  97.3 5.3 %all-to-all-done.6.values = f32[32,8,128]{2,1,0:T(8,128)S(1)} async-done(((f32[32,8,128]{2,1,0:T(8,128)}), f32[32,8,128]{2,1,0:T(8,128)S(1)}, u32[]{:S(2)}, u32[]{:S(2)}) %all-to-all-start.6) | async-done | bytes 131104 | tf_op jit(solution)/shard_map/all_to_all | solution.py:432
  102.6 0.8 finish.1
  (1 shorter events, 0.0 us)
Async XLA Ops:
  0.6 10.2 %copy-start.2 = (bf16[32,864]{1,0:T(8,128)(2,1)S(1)}, bf16[32,864]{1,0:T(8,128)(2,1)}, u32[]{:S(2)}) copy-start(bf16[32,864]{1,0:T(8,128)(2,1)} %conv_w.3) | copy-start | bytes 165892
  2.1 8.8 %copy-start.4 = (bf16[32,64]{1,0:T(8,128)(2,1)S(1)}, bf16[32,64]{1,0:T(8,128)(2,1)}, u32[]{:S(2)}) copy-start(bf16[32,64]{1,0:T(8,128)(2,1)} %w1.3) | copy-start | bytes 12292
  2.1 16.0 %all-to-all-start = ((s32[32,1,256]{2,1,0:T(1,128)}), s32[32,1,256]{2,1,0:T(1,128)S(1)}, u32[]{:S(2)}, u32[]{:S(2)}) async-start(s32[32,1,256]{2,1,0:T(1,128)} %reshape_squeeze.3), calls=%async_computation | async-start | bytes 65536 | tf_op jit(solution)/shard_map/all_to_all | solution.py:432
  10.8 0.7 copy-start.10
  10.8 0.7 copy-start.8
  10.8 0.7 copy-start.9
  11.5 1.0 copy-start
  19.7 6.1 %copy-start.3 = (s32[1,4096]{1,0:T(1,128)S(1)}, s32[1,4096]{1,0:T(1,128)}, u32[]{:S(2)}) copy-start(s32[1,4096]{1,0:T(1,128)} %sources) | copy-start | bytes 49156
  19.7 6.1 %copy-start.6 = (f32[512]{0:T(512)S(1)}, f32[512]{0:T(512)}, u32[]{:S(2)}) copy-start(f32[512]{0:T(512)} %param.20) | copy-start | bytes 6148
  19.7 6.1 %copy-start.7 = (s32[512]{0:T(512)S(1)}, s32[512]{0:T(512)}, u32[]{:S(2)}) copy-start(s32[512]{0:T(512)} %param.21) | copy-start | bytes 6148
  19.7 13.4 %all-to-all-start.1 = ((f32[32,4,128]{2,1,0:T(4,128)}), f32[32,4,128]{2,1,0:T(4,128)S(1)}, u32[]{:S(2)}, u32[]{:S(2)}) async-start(f32[32,4,128]{2,1,0:T(4,128)} %owner_pick.1), calls=%async_computation.1 | async-start | bytes 131072 | tf_op jit(solution)/shard_map/all_to_all | solution.py:432
  25.7 0.7 copy-start.5
  49.2 13.6 %copy-start.1 = (bf16[1,8,32,512]{3,2,1,0:T(8,128)(2,1)S(1)}, bf16[1,8,32,512]{3,2,1,0:T(8,128)(2,1)}, u32[]{:S(2)}) copy-start(bf16[1,8,32,512]{3,2,1,0:T(8,128)(2,1)} %param.11) | copy-start | bytes 786436
  89.7 12.9 %all-to-all-start.6 = ((f32[32,8,128]{2,1,0:T(8,128)}), f32[32,8,128]{2,1,0:T(8,128)S(1)}, u32[]{:S(2)}, u32[]{:S(2)}) async-start(f32[32,8,128]{2,1,0:T(8,128)} %add_shells.1), calls=%async_computation.6 | async-start | bytes 262144 | tf_op jit(solution)/shard_map/all_to_all | solution.py:432

commit v3 on v2

--- a/solution.py
+++ b/solution.py
@@ -14,6 +14,8 @@
 GELU_C = 0.7978845608028654
 GELU_A = 0.044715
 
+M_DECODE, M_BACK, M_GRAD, U_SPREAD = 8, 8, 4, 16
+
 F32 = jnp.float32
 BF16 = jnp.bfloat16
 NT = (((1,), (1,)), ((), ()))
@@ -69,7 +71,7 @@
 def shift_cells(x, direction, stride):
     if direction == 0:
         return x
-    pos = (iota((1, CELLS), 1) // stride) & 7
+    pos = (iota((1, x.shape[1]), 1) // stride) & 7
     ok = (pos >= 1) if direction < 0 else (pos <= 6)
     return jnp.where(ok, moved(x, direction * stride), 0.0)
 
@@ -107,14 +109,20 @@
     return jnp.concatenate(rows, axis=0).astype(BF16)
 
 
+def side_by_side(bricks, first, number):
+    return jnp.concatenate([bricks[first + n] for n in range(number)], axis=1)
+
+
 def decode_kernel(bricks, conv_w, conv_b, w1, b1, w2t, dec_out, slope_out, planes_out, factor_out, e0_s, e1_s):
     count, ch = bricks.shape[0], bricks.shape[1]
     bias = column(conv_b[...])
     bias1 = column(b1[...])
     w2_0, w2_1 = column(w2t[0:1, :]), column(w2t[1:2, :])
     wf = offset_rows(conv_w)
-    for n in range(count):
-        y = dot(wf, c_columns(bricks[n]))
+
+    for first in range(0, count, M_DECODE):
+        cells = slice(first * CELLS, (first + M_DECODE) * CELLS)
+        y = dot(wf, c_columns(side_by_side(bricks, first, M_DECODE)))
         pre = bias
         for a in range(3):
             rows = [y[(3 * a + b) * ch : (3 * a + b + 1) * ch] for b in range(3)]
@@ -122,15 +130,14 @@
             pre = pre + shift_cells(t, a - 1, 64)
         value, slope = gelu_pair(pre)
         dec = value.astype(BF16)
-        dec_out[:, n * CELLS : (n + 1) * CELLS] = dec
-        slope_out[:, n * CELLS : (n + 1) * CELLS] = slope
+        dec_out[:, cells] = dec
+        slope_out[:, cells] = slope
         g = gelu_pair(dot(w1[...], dec, TN) + bias1)[0]
-        e0 = jnp.sum(w2_0 * g, axis=0, keepdims=True)
-        e1 = jnp.sum(w2_1 * g, axis=0, keepdims=True)
-        for half in range(CELLS // HI):
-            at = n * (CELLS // HI) + half
-            e0_s[at : at + 1, :] = e0[:, half * HI : (half + 1) * HI]
-            e1_s[at : at + 1, :] = e1[:, half * HI : (half + 1) * HI]
+        for w, e_s in ((w2_0, e0_s), (w2_1, e1_s)):
+            e = jnp.sum(w * g, axis=0, keepdims=True)
+            for k in range(M_DECODE * CELLS // HI):
+                at = first * (CELLS // HI) + k
+                e_s[at : at + 1, :] = e[:, k * HI : (k + 1) * HI]
     e0 = e0_s[...]
     e1 = e1_s[...]
     density = jnp.maximum(e0, 0.0) + jnp.log1p(jnp.exp(-jnp.abs(e0)))
@@ -161,6 +168,11 @@
     targets_out[1:2, :] = inten_target[...]
     targets_out[2:3, :] = drop[...].astype(F32)
     slots_out[...] = rays_last(sources)
+
+
+def queries_kernel(queries, bricks, conv_w, conv_b, w1, b1, w2t, out):
+    for s in range(out.shape[0]):
+        out[s] = queries[s : s + 1, :]
 
 
 def one_hot(low):
@@ -302,7 +314,7 @@
 
 
 def owner_back_kernel(
-    addr, cots, factor, dec, slope, bricks, w1, b1, w2t, loss, payload_out, cot_out, plane_s
+    addr, cots, factor, dec, slope, bricks, w1, b1, w2t, loss, payload_out, cot_out, plane_s, ge_s
 ):
     count, ch = bricks.shape[0], bricks.shape[1]
     hid = w1.shape[1]
@@ -316,22 +328,24 @@
     def body(s, acc):
         return acc + spread([plane_s[k, pl.ds(s, 1), :] for k in range(6)], groups, addr[s])
 
-    acc = lax.fori_loop(0, sectors, body, jnp.zeros((6 * groups, HI), F32), unroll=16)
+    acc = lax.fori_loop(0, sectors, body, jnp.zeros((6 * groups, HI), F32), unroll=U_SPREAD)
     pair = join_planes(acc, groups)
-    ge = [pair[v] * factor[v] for v in range(2)]
+    for v in range(2):
+        ge_s[v] = pair[v] * factor[v]
     bias1 = column(b1[...])
     w2_0, w2_1 = column(w2t[0:1, :]), column(w2t[1:2, :])
     per = CELLS // HI
+
     acc_w1 = jnp.zeros((ch, hid), F32)
     acc_b1 = jnp.zeros((hid, LANE), F32)
     acc_w20 = jnp.zeros((hid, LANE), F32)
     acc_w21 = jnp.zeros((hid, LANE), F32)
     acc_cb = jnp.zeros((ch, LANE), F32)
     acc_cw = jnp.zeros((9 * ch, 3 * ch), F32)
-    for n in range(count):
-        cells = slice(n * CELLS, (n + 1) * CELLS)
+    for first in range(0, count, M_BACK):
+        cells = slice(first * CELLS, (first + M_BACK) * CELLS)
         rows = [
-            jnp.concatenate([ge[v][n * per + k : n * per + k + 1] for k in range(per)], axis=1)
+            jnp.concatenate([ge_s[v, first * per + k : first * per + k + 1, :] for k in range(M_BACK * per)], axis=1)
             for v in range(2)
         ]
         dec_n = dec[:, cells]
@@ -347,7 +361,7 @@
         cot_out[:, cells] = cot
         wide = cot.astype(F32)
         acc_cb = acc_cb + fold_lanes(wide)
-        acc_cw = acc_cw + dot(ab_columns(wide), c_columns(bricks[n]), NT)
+        acc_cw = acc_cw + dot(ab_columns(wide), c_columns(side_by_side(bricks, first, M_BACK)), NT)
     lane = iota((ch, LANE), 1)
     tiles = [jnp.zeros((ch, LANE), F32) for _ in range(7)]
     pad = jnp.zeros((ch, LANE - 3 * ch), F32)
@@ -379,12 +393,13 @@
 def bricks_back_kernel(cot, conv_w, out):
     count, ch = out.shape[0], out.shape[1]
     wf = offset_rows(conv_w)
-    for n in range(count):
-        wide = cot[:, n * CELLS : (n + 1) * CELLS].astype(F32)
+    for first in range(0, count, M_GRAD):
+        wide = cot[:, first * CELLS : (first + M_GRAD) * CELLS].astype(F32)
         z = dot(wf, ab_columns(wide), TN)
         total = z[ch : 2 * ch]
         total = total + shift_cells(z[0:ch], 1, 1) + shift_cells(z[2 * ch : 3 * ch], -1, 1)
-        out[n] = total.astype(BF16)
+        for n in range(M_GRAD):
+            out[first + n] = total[:, n * CELLS : (n + 1) * CELLS].astype(BF16)
 
 
 def add_kernel(values, out):
@@ -444,14 +459,23 @@
     cells = count * CELLS
     groups = cells // HI
     rays = depth_target.shape[0]
-    addr = swap(queries[0].reshape(sectors, 1, HI), "sector")
     b1 = head_b1.reshape(1, hid)
     w2t = head_w2.T
+    operands = (blocks, conv_w, conv_b.reshape(1, ch), head_w1, b1, w2t)
+    (asked,) = call(
+        queries_kernel,
+        [((sectors, 1, HI), jnp.int32)],
+        [VMEM] * 7,
+        (queries[0],) + operands,
+        name="queries",
+        moved_bytes=10**6,
+    )
+    addr = swap(asked, "sector")
     dec, slope, planes, factor = call(
         decode_kernel,
         [((ch, cells), BF16), ((ch, cells), F32), ((6 * groups, HI), BF16), ((2, groups, HI), F32)],
         [VMEM] * 6,
-        (blocks, conv_w, conv_b.reshape(1, ch), head_w1, b1, w2t),
+        operands,
         scratch=[pltpu.VMEM((groups, HI), F32), pltpu.VMEM((groups, HI), F32)],
         name="decode",
         flops=2 * 10**9,
@@ -506,7 +530,7 @@
         [((ch, 8, LANE), F32), ((ch, cells), BF16)],
         [VMEM] * 10,
         (addr, cots, factor, dec, slope, blocks, head_w1, b1, w2t, loss),
-        scratch=[pltpu.VMEM((6, sectors, HI), F32)],
+        scratch=[pltpu.VMEM((6, sectors, HI), F32), pltpu.VMEM((2, groups, HI), F32)],
         name="owner_back",
         flops=2 * 10**9,
         moved_bytes=2 * 10**6,

time: 104 us -> 105 us (level)
  waiting for transfers between devices: 13.2 us -> 16.8 us
  starting transfers between devices: 19.8 us -> 17.8 us
  Pallas kernels: 17.9 us -> 16 us
  local copies, waits for them, and re-layouts: 3.69 us -> 5.19 us
    all_to_all x3, waiting for transfers between devices: 13.2 us -> 16.8 us  [swap(): return lax.all_to_all(value, axis, split_axis=0, concat_axis=0, tiled=True)]
    unnamed x22 -> x30, local copies, waits for them, and re-layouts: 2.28 us -> 5.19 us
    all_to_all x3, starting transfers between devices: 19.8 us -> 17.8 us  [swap(): return lax.all_to_all(value, axis, split_axis=0, concat_axis=0, tiled=True)]
    pallas_call x10 -> x11, Pallas kernels: 17.9 us -> 16 us  [call(): pl.pallas_call(kernel, out_shape=shapes, in_specs=specs, out_specs=out_sp...]
    another operation x1 -> x0, local copies, waits for them, and re-layouts: 1.41 us -> none  [local(): addr = swap(queries[0].reshape(sectors, 1, HI), 'sector')]
  transfers between devices with their start and end apart: 3 -> 3, of which waited for: 3 -> 3; matrix products, arithmetic and copies ran while one was open for 0% -> 0% of each run, Pallas kernels for 7% -> 5%
where the time goes in v3:
time: 105 us
  blocking collectives  47.9 us (46%)
  starting transfers between devices  17.8 us (17%)
  waiting for transfers between devices  16.8 us (16%)
  Pallas kernels  16 us (15%)
  local copies, waits for them, and re-layouts  5.19 us (5%)
    all_to_all x4, blocking collectives, swap(): return lax.all_to_all(value, axis, split_axis=0, concat_axis=0, tiled=True)  47.9 us
    all_to_all x3, starting transfers between devices, swap(): return lax.all_to_all(value, axis, split_axis=0, concat_axis=0, tiled=True)  17.8 us
    all_to_all x3, waiting for transfers between devices, swap(): return lax.all_to_all(value, axis, split_axis=0, concat_axis=0, tiled=True)  16.8 us
    pallas_call x11, Pallas kernels, call(): pl.pallas_call(kernel, out_shape=shapes, in_specs=specs, out_specs=out_sp...  16 us
    unnamed x30, local copies, waits for them, and re-layouts  5.19 us
  transfers between devices with their start and end apart: 3, of which 3 were waited for; matrix products, arithmetic and copies ran while one was open for 0% of the time, Pallas kernels for 5%

profile of v3, /device:TPU:1, one launch (start us, length us, event | category | flops | bytes accessed | tf_op | source)
XLA Modules:
  0.0 104.5 jit_solution(12539703819294478965)
XLA Ops:
  0.6 0.0 copy-start.5
  0.6 0.0 copy-start.6
  0.7 0.7 copy-done.5
  1.3 0.0 copy-done.6
  1.3 0.0 copy-start
  1.3 0.9 copy-done
  2.3 0.0 copy-start.2
  2.3 0.8 copy-done.2
  3.1 0.0 copy-start.4
  3.1 0.8 copy-done.4
  3.9 0.0 copy-start.7
  3.9 0.7 copy-done.7
  4.5 0.0 copy-start.9
  4.5 0.7 copy-done.9
  5.2 0.0 copy-start.1
  5.2 0.6 queries.1
  5.8 0.0 copy-start.3
  5.8 0.0 copy-start.8
  5.8 0.0 copy-start.10
  5.8 8.7 %all-to-all-start = ((s32[32,1,256]{2,1,0:T(1,128)}), s32[32,1,256]{2,1,0:T(1,128)S(1)}, u32[]{:S(2)}, u32[]{:S(2)}) async-start(s32[32,1,256]{2,1,0:T(1,128)} %queries.1), calls=%async_computation | async-start | bytes 65536 | tf_op jit(solution)/shard_map/all_to_all | solution.py:447
  14.5 0.0 copy-done.1
  14.6 0.0 copy-done.3
  14.6 0.0 copy-done.8
  14.6 0.0 copy-done.10
  14.6 2.6 %decode.1 = (bf16[32,4096]{1,0:T(8,128)(2,1)S(1)}, f32[32,4096]{1,0:T(8,128)S(1)}, bf16[96,256]{1,0:T(8,128)(2,1)S(1)}, f32[2,16,256]{2,1,0:T(8,128)S(1)}) custom-call(bf16[8,32,512]{2,1,0:T(8,128)(2,1)S(1)} %bitcast.16, bf16[32,864]{1,0:T(8,128)(2,1)S(1)} %copy-done.3, f32[1,32]{1,0:T(1,128)S(1)} %bitcast.23, bf16[32,64]{1,0:T(8,128)(2,1)S(1)} %copy-done.5, ...), custom_call_target="tpu_custom_call" | custom-call | flops 2000000000 | bytes 2000000 | tf_op jit(solution)/shard_map/decode/pallas_call | solution.py:434
  17.2 4.7 %all-to-all-done.addr = s32[32,1,256]{2,1,0:T(1,128)S(1)} async-done(((s32[32,1,256]{2,1,0:T(1,128)}), s32[32,1,256]{2,1,0:T(1,128)S(1)}, u32[]{:S(2)}, u32[]{:S(2)}) %all-to-all-start) | async-done | bytes 32800 | tf_op jit(solution)/shard_map/all_to_all | solution.py:447
  21.8 1.6 %owner_pick.1 = f32[32,4,128]{2,1,0:T(4,128)} custom-call(s32[32,1,256]{2,1,0:T(1,128)S(1)} %all-to-all-done.addr, bf16[96,256]{1,0:T(8,128)(2,1)S(1)} %get-tuple-element.29.planes), custom_call_target="tpu_custom_call" | custom-call | flops 1000000000 | bytes 100000 | tf_op jit(solution)/shard_map/owner_pick/pallas_call | solution.py:434
  23.4 0.0 copy-start.11
  23.4 0.0 copy-start.13
  23.4 0.0 copy-start.14
  23.4 4.0 %all-to-all-start.1 = ((f32[32,4,128]{2,1,0:T(4,128)}), f32[32,4,128]{2,1,0:T(4,128)S(1)}, u32[]{:S(2)}, u32[]{:S(2)}) async-start(f32[32,4,128]{2,1,0:T(4,128)} %owner_pick.1), calls=%async_computation.1 | async-start | bytes 131072 | tf_op jit(solution)/shard_map/all_to_all | solution.py:447
  27.5 0.0 copy-start.12
  27.5 0.0 copy-done.11
  27.5 0.0 copy-done.13
  27.5 0.0 copy-done.14
  27.5 0.6 copy-done.12
  28.2 0.3 arrange.1
  28.4 6.5 %all-to-all-done.1.replies = f32[32,4,128]{2,1,0:T(4,128)S(1)} async-done(((f32[32,4,128]{2,1,0:T(4,128)}), f32[32,4,128]{2,1,0:T(4,128)S(1)}, u32[]{:S(2)}, u32[]{:S(2)}) %all-to-all-start.1) | async-done | bytes 65568 | tf_op jit(solution)/shard_map/all_to_all | solution.py:447
  35.0 0.9 sample.1
  35.9 15.2 %all_to_all.35.terms = f32[8,4,512]{2,1,0:T(4,128)S(1)} all-to-all(f32[8,4,512]{2,1,0:T(4,128)S(1)} %get-tuple-element.32), channel_id=1, replica_groups=mesh['shell'=8,'sector'=32] {'shell'}, dimensions={0} | all-to-all | bytes 131072 | tf_op jit(solution)/shard_map/all_to_all | solution.py:447
  51.1 1.3 %render.1 = (f32[32,4,128]{2,1,0:T(4,128)S(1)}, f32[1,512]{1,0:T(1,128)}, f32[1,1]{1,0:T(1,128)}) custom-call(s32[1]{0:T(128)} %bitcast.5.shell_ref, f32[8,4,512]{2,1,0:T(4,128)S(1)} %all_to_all.35.terms, f32[8,512]{1,0:T(8,128)S(1)} %get-tuple-element.33.density, f32[8,512]{1,0:T(8,128)S(1)} %get-tuple-element.34.intensity, ...), custom_call_target="tpu_custom_call" | custom-call | flops 1000000000 | bytes 100000 | tf_op jit(solution)/shard_map/render/pallas_call | solution.py:434
  52.4 12.3 %all_to_all.36.cots = f32[32,4,128]{2,1,0:T(4,128)S(1)} all-to-all(f32[32,4,128]{2,1,0:T(4,128)S(1)} %get-tuple-element.36), channel_id=1, replica_groups=mesh['shell'=8,'sector'=32] {'sector'}, dimensions={0} | all-to-all | bytes 131072 | tf_op jit(solution)/shard_map/all_to_all | solution.py:447
  64.7 5.1 %owner_back.1 = (f32[32,8,128]{2,1,0:T(8,128)S(1)}, bf16[32,4096]{1,0:T(8,128)(2,1)S(1)}) custom-call(s32[32,1,256]{2,1,0:T(1,128)S(1)} %all-to-all-done.addr, f32[32,4,128]{2,1,0:T(4,128)S(1)} %all_to_all.36.cots, f32[2,16,256]{2,1,0:T(8,128)S(1)} %get-tuple-element.37.factor, bf16[32,4096]{1,0:T(8,128)(2,1)S(1)} %get-tuple-element.38.dec, ...), custom_call_target="tpu_custom_call" | custom-call | flops 2000000000 | bytes 2000000 | tf_op jit(solution)/shard_map/owner_back/pallas_call | solution.py:434
  69.8 11.2 %all_to_all.37.values = f32[32,8,128]{2,1,0:T(8,128)S(1)} all-to-all(f32[32,8,128]{2,1,0:T(8,128)S(1)} %get-tuple-element.41), channel_id=1, replica_groups=mesh['shell'=8,'sector'=32] {'sector'}, dimensions={0} | all-to-all | bytes 262144 | tf_op jit(solution)/shard_map/all_to_all | solution.py:447
  81.0 9.2 %all_to_all.38.values = f32[8,8,128]{2,1,0:T(8,128)S(1)} all-to-all(f32[8,8,128]{2,1,0:T(8,128)S(1)} %add_sectors.1), channel_id=1, replica_groups=mesh['shell'=8,'sector'=32] {'shell'}, dimensions={0} | all-to-all | bytes 65536 | tf_op jit(solution)/shard_map/all_to_all | solution.py:447
  90.2 0.7 add_shells.1
  90.9 5.1 %all-to-all-start.6 = ((f32[32,8,128]{2,1,0:T(8,128)}), f32[32,8,128]{2,1,0:T(8,128)S(1)}, u32[]{:S(2)}, u32[]{:S(2)}) async-start(f32[32,8,128]{2,1,0:T(8,128)} %add_shells.1), calls=%async_computation.6 | async-start | bytes 262144 | tf_op jit(solution)/shard_map/all_to_all | solution.py:447
  96.0 2.2 %bricks_back.1 = bf16[8,32,512]{2,1,0:T(8,128)(2,1)} custom-call(bf16[32,4096]{1,0:T(8,128)(2,1)S(1)} %get-tuple-element.48.cot, bf16[32,864]{1,0:T(8,128)(2,1)S(1)} %copy-done.3), custom_call_target="tpu_custom_call" | custom-call | flops 2000000000 | bytes 1000000 | tf_op jit(solution)/shard_map/bricks_back/pallas_call | solution.py:434
  98.2 5.6 %all-to-all-done.6.values = f32[32,8,128]{2,1,0:T(8,128)S(1)} async-done(((f32[32,8,128]{2,1,0:T(8,128)}), f32[32,8,128]{2,1,0:T(8,128)S(1)}, u32[]{:S(2)}, u32[]{:S(2)}) %all-to-all-start.6) | async-done | bytes 131104 | tf_op jit(solution)/shard_map/all_to_all | solution.py:447
  103.8 0.8 finish.1
  (1 shorter events, 0.0 us)
Async XLA Ops:
  0.6 0.7 copy-start.5
  0.6 0.7 copy-start.6
  1.3 1.0 copy-start
  2.3 0.8 copy-start.2
  3.1 0.8 copy-start.4
  3.9 0.7 copy-start.7
  4.5 0.7 copy-start.9
  5.2 9.4 %copy-start.1 = (bf16[1,8,32,512]{3,2,1,0:T(8,128)(2,1)S(1)}, bf16[1,8,32,512]{3,2,1,0:T(8,128)(2,1)}, u32[]{:S(2)}) copy-start(bf16[1,8,32,512]{3,2,1,0:T(8,128)(2,1)} %param.11) | copy-start | bytes 786436
  5.8 8.7 %copy-start.3 = (bf16[32,864]{1,0:T(8,128)(2,1)S(1)}, bf16[32,864]{1,0:T(8,128)(2,1)}, u32[]{:S(2)}) copy-start(bf16[32,864]{1,0:T(8,128)(2,1)} %conv_w.5) | copy-start | bytes 165892
  5.8 8.8 %copy-start.8 = (f32[32]{0:T(128)S(1)}, f32[32]{0:T(128)}, u32[]{:S(2)}) copy-start(f32[32]{0:T(128)} %param.13) | copy-start | bytes 388
  5.8 8.8 %copy-start.10 = (f32[64]{0:T(128)S(1)}, f32[64]{0:T(128)}, u32[]{:S(2)}) copy-start(f32[64]{0:T(128)} %param.15) | copy-start | bytes 772
  5.8 16.0 %all-to-all-start = ((s32[32,1,256]{2,1,0:T(1,128)}), s32[32,1,256]{2,1,0:T(1,128)S(1)}, u32[]{:S(2)}, u32[]{:S(2)}) async-start(s32[32,1,256]{2,1,0:T(1,128)} %queries.1), calls=%async_computation | async-start | bytes 65536 | tf_op jit(solution)/shard_map/all_to_all | solution.py:447
  23.4 4.1 %copy-start.11 = (s32[1,4096]{1,0:T(1,128)S(1)}, s32[1,4096]{1,0:T(1,128)}, u32[]{:S(2)}) copy-start(s32[1,4096]{1,0:T(1,128)} %sources) | copy-start | bytes 49156
  23.4 4.1 %copy-start.13 = (f32[512]{0:T(512)S(1)}, f32[512]{0:T(512)}, u32[]{:S(2)}) copy-start(f32[512]{0:T(512)} %param.20) | copy-start | bytes 6148
  23.4 4.1 %copy-start.14 = (s32[512]{0:T(512)S(1)}, s32[512]{0:T(512)}, u32[]{:S(2)}) copy-start(s32[512]{0:T(512)} %param.21) | copy-start | bytes 6148
  23.4 11.5 %all-to-all-start.1 = ((f32[32,4,128]{2,1,0:T(4,128)}), f32[32,4,128]{2,1,0:T(4,128)S(1)}, u32[]{:S(2)}, u32[]{:S(2)}) async-start(f32[32,4,128]{2,1,0:T(4,128)} %owner_pick.1), calls=%async_computation.1 | async-start | bytes 131072 | tf_op jit(solution)/shard_map/all_to_all | solution.py:447
  27.5 0.7 copy-start.12
  90.9 12.9 %all-to-all-start.6 = ((f32[32,8,128]{2,1,0:T(8,128)}), f32[32,8,128]{2,1,0:T(8,128)S(1)}, u32[]{:S(2)}, u32[]{:S(2)}) async-start(f32[32,8,128]{2,1,0:T(8,128)} %add_shells.1), calls=%async_computation.6 | async-start | bytes 262144 | tf_op jit(solution)/shard_map/all_to_all | solution.py:447

commit v4 on v3

--- a/solution.py
+++ b/solution.py
@@ -168,11 +168,6 @@
     targets_out[1:2, :] = inten_target[...]
     targets_out[2:3, :] = drop[...].astype(F32)
     slots_out[...] = rays_last(sources)
-
-
-def queries_kernel(queries, bricks, conv_w, conv_b, w1, b1, w2t, out):
-    for s in range(out.shape[0]):
-        out[s] = queries[s : s + 1, :]
 
 
 def one_hot(low):
@@ -462,15 +457,7 @@
     b1 = head_b1.reshape(1, hid)
     w2t = head_w2.T
     operands = (blocks, conv_w, conv_b.reshape(1, ch), head_w1, b1, w2t)
-    (asked,) = call(
-        queries_kernel,
-        [((sectors, 1, HI), jnp.int32)],
-        [VMEM] * 7,
-        (queries[0],) + operands,
-        name="queries",
-        moved_bytes=10**6,
-    )
-    addr = swap(asked, "sector")
+    addr = swap(queries[0].reshape(sectors, 1, HI), "sector")
     dec, slope, planes, factor = call(
         decode_kernel,
         [((ch, cells), BF16), ((ch, cells), F32), ((6 * groups, HI), BF16), ((2, groups, HI), F32)],

time: 105 us -> 102 us (0.971)
  waiting for transfers between devices: 16.8 us -> 15.1 us
  local copies, waits for them, and re-layouts: 5.19 us -> 3.69 us
    unnamed x30 -> x22, local copies, waits for them, and re-layouts: 5.19 us -> 2.28 us
    all_to_all x3, waiting for transfers between devices: 16.8 us -> 15.1 us  [swap(): return lax.all_to_all(value, axis, split_axis=0, concat_axis=0, tiled=True)]
    another operation x0 -> x1, local copies, waits for them, and re-layouts: none -> 1.41 us  [local(): addr = swap(queries[0].reshape(sectors, 1, HI), 'sector')]
    pallas_call x11 -> x10, Pallas kernels: 16 us -> 15.4 us  [call(): pl.pallas_call(kernel, out_shape=shapes, in_specs=specs, out_specs=out_sp...]
where the time goes in v4:
time: 102 us; the launch traced here: 101 us
  blocking collectives  47.9 us (47%)
  starting transfers between devices  18.2 us (18%)
  Pallas kernels  15.4 us (15%)
  waiting for transfers between devices  15.1 us (15%)
  local copies, waits for them, and re-layouts  3.69 us (4%)
    all_to_all x4, blocking collectives, swap(): return lax.all_to_all(value, axis, split_axis=0, concat_axis=0, tiled=True)  47.9 us
    all_to_all x3, starting transfers between devices, swap(): return lax.all_to_all(value, axis, split_axis=0, concat_axis=0, tiled=True)  18.2 us
    pallas_call x10, Pallas kernels, call(): pl.pallas_call(kernel, out_shape=shapes, in_specs=specs, out_specs=out_sp...  15.4 us
    all_to_all x3, waiting for transfers between devices, swap(): return lax.all_to_all(value, axis, split_axis=0, concat_axis=0, tiled=True)  15.1 us
    unnamed x22, local copies, waits for them, and re-layouts  2.28 us
  transfers between devices with their start and end apart: 3, of which 3 were waited for; matrix products, arithmetic and copies ran while one was open for 0% of the time, Pallas kernels for 5%

profile of v4, /device:TPU:1, one launch (start us, length us, event | category | flops | bytes accessed | tf_op | source)
XLA Modules:
  0.0 101.1 jit_solution(5659474964598573884)
XLA Ops:
  0.6 0.0 copy-start.2
  0.6 1.4 %reshape_squeeze.3 = s32[32,1,256]{2,1,0:T(1,128)} reshape(s32[1,32,256]{2,1,0:T(8,128)} %param.17) | data formatting | bytes 65536 | tf_op jit(solution)/shard_map/reshape;squeeze | solution.py:460
  2.1 0.0 copy-start.4
  2.1 8.7 %all-to-all-start = ((s32[32,1,256]{2,1,0:T(1,128)}), s32[32,1,256]{2,1,0:T(1,128)S(1)}, u32[]{:S(2)}, u32[]{:S(2)}) async-start(s32[32,1,256]{2,1,0:T(1,128)} %reshape_squeeze.3), calls=%async_computation | async-start | bytes 65536 | tf_op jit(solution)/shard_map/all_to_all | solution.py:442
  10.8 0.0 copy-start.10
  10.8 0.0 copy-start.8
  10.8 0.0 copy-start.9
  10.8 0.0 copy-done.2
  10.8 0.0 copy-done.4
  10.8 0.6 copy-done.10
  11.4 0.0 copy-done.8
  11.5 0.0 copy-done.9
  11.5 0.0 copy-start
  11.5 0.9 copy-done
  12.4 2.6 %decode.1 = (bf16[32,4096]{1,0:T(8,128)(2,1)S(1)}, f32[32,4096]{1,0:T(8,128)S(1)}, bf16[96,256]{1,0:T(8,128)(2,1)S(1)}, f32[2,16,256]{2,1,0:T(8,128)S(1)}) custom-call(bf16[8,32,512]{2,1,0:T(8,128)(2,1)S(1)} %bitcast.14, bf16[32,864]{1,0:T(8,128)(2,1)S(1)} %copy-done.2, f32[1,32]{1,0:T(1,128)S(1)} %bitcast.21, bf16[32,64]{1,0:T(8,128)(2,1)S(1)} %copy-done.4, ...), custom_call_target="tpu_custom_call" | custom-call | flops 2000000000 | bytes 2000000 | tf_op jit(solution)/shard_map/decode/pallas_call | solution.py:429
  15.0 3.0 %all-to-all-done.addr = s32[32,1,256]{2,1,0:T(1,128)S(1)} async-done(((s32[32,1,256]{2,1,0:T(1,128)}), s32[32,1,256]{2,1,0:T(1,128)S(1)}, u32[]{:S(2)}, u32[]{:S(2)}) %all-to-all-start) | async-done | bytes 32800 | tf_op jit(solution)/shard_map/all_to_all | solution.py:442
  18.1 1.6 %owner_pick.1 = f32[32,4,128]{2,1,0:T(4,128)} custom-call(s32[32,1,256]{2,1,0:T(1,128)S(1)} %all-to-all-done.addr, bf16[96,256]{1,0:T(8,128)(2,1)S(1)} %get-tuple-element.29.planes), custom_call_target="tpu_custom_call" | custom-call | flops 1000000000 | bytes 100000 | tf_op jit(solution)/shard_map/owner_pick/pallas_call | solution.py:429
  19.7 0.0 copy-start.3
  19.7 0.0 copy-start.6
  19.7 0.0 copy-start.7
  19.7 4.5 %all-to-all-start.1 = ((f32[32,4,128]{2,1,0:T(4,128)}), f32[32,4,128]{2,1,0:T(4,128)S(1)}, u32[]{:S(2)}, u32[]{:S(2)}) async-start(f32[32,4,128]{2,1,0:T(4,128)} %owner_pick.1), calls=%async_computation.1 | async-start | bytes 131072 | tf_op jit(solution)/shard_map/all_to_all | solution.py:442
  24.2 0.0 copy-start.5
  24.2 0.0 copy-done.3
  24.2 0.0 copy-done.6
  24.2 0.0 copy-done.7
  24.2 0.6 copy-done.5
  24.8 0.3 arrange.1
  25.1 6.4 %all-to-all-done.1.replies = f32[32,4,128]{2,1,0:T(4,128)S(1)} async-done(((f32[32,4,128]{2,1,0:T(4,128)}), f32[32,4,128]{2,1,0:T(4,128)S(1)}, u32[]{:S(2)}, u32[]{:S(2)}) %all-to-all-start.1) | async-done | bytes 65568 | tf_op jit(solution)/shard_map/all_to_all | solution.py:442
  31.5 0.9 sample.1
  32.4 15.2 %all_to_all.35.terms = f32[8,4,512]{2,1,0:T(4,128)S(1)} all-to-all(f32[8,4,512]{2,1,0:T(4,128)S(1)} %get-tuple-element.32), channel_id=1, replica_groups=mesh['shell'=8,'sector'=32] {'shell'}, dimensions={0} | all-to-all | bytes 131072 | tf_op jit(solution)/shard_map/all_to_all | solution.py:442
  47.7 0.0 copy-start.1
  47.7 1.3 %render.1 = (f32[32,4,128]{2,1,0:T(4,128)S(1)}, f32[1,512]{1,0:T(1,128)}, f32[1,1]{1,0:T(1,128)}) custom-call(s32[1]{0:T(128)} %bitcast.shell_ref, f32[8,4,512]{2,1,0:T(4,128)S(1)} %all_to_all.35.terms, f32[8,512]{1,0:T(8,128)S(1)} %get-tuple-element.33.density, f32[8,512]{1,0:T(8,128)S(1)} %get-tuple-element.34.intensity, ...), custom_call_target="tpu_custom_call" | custom-call | flops 1000000000 | bytes 100000 | tf_op jit(solution)/shard_map/render/pallas_call | solution.py:429
  49.0 12.3 %all_to_all.36.cots = f32[32,4,128]{2,1,0:T(4,128)S(1)} all-to-all(f32[32,4,128]{2,1,0:T(4,128)S(1)} %get-tuple-element.36), channel_id=1, replica_groups=mesh['shell'=8,'sector'=32] {'sector'}, dimensions={0} | all-to-all | bytes 131072 | tf_op jit(solution)/shard_map/all_to_all | solution.py:442
  61.3 0.0 copy-done.1
  61.3 5.1 %owner_back.1 = (f32[32,8,128]{2,1,0:T(8,128)S(1)}, bf16[32,4096]{1,0:T(8,128)(2,1)S(1)}) custom-call(s32[32,1,256]{2,1,0:T(1,128)S(1)} %all-to-all-done.addr, f32[32,4,128]{2,1,0:T(4,128)S(1)} %all_to_all.36.cots, f32[2,16,256]{2,1,0:T(8,128)S(1)} %get-tuple-element.37.factor, bf16[32,4096]{1,0:T(8,128)(2,1)S(1)} %get-tuple-element.38.dec, ...), custom_call_target="tpu_custom_call" | custom-call | flops 2000000000 | bytes 2000000 | tf_op jit(solution)/shard_map/owner_back/pallas_call | solution.py:429
  66.3 11.2 %all_to_all.37.values = f32[32,8,128]{2,1,0:T(8,128)S(1)} all-to-all(f32[32,8,128]{2,1,0:T(8,128)S(1)} %get-tuple-element.41), channel_id=1, replica_groups=mesh['shell'=8,'sector'=32] {'sector'}, dimensions={0} | all-to-all | bytes 262144 | tf_op jit(solution)/shard_map/all_to_all | solution.py:442
  77.6 9.2 %all_to_all.38.values = f32[8,8,128]{2,1,0:T(8,128)S(1)} all-to-all(f32[8,8,128]{2,1,0:T(8,128)S(1)} %add_sectors.1), channel_id=1, replica_groups=mesh['shell'=8,'sector'=32] {'shell'}, dimensions={0} | all-to-all | bytes 65536 | tf_op jit(solution)/shard_map/all_to_all | solution.py:442
  86.8 0.7 add_shells.1
  87.5 5.0 %all-to-all-start.6 = ((f32[32,8,128]{2,1,0:T(8,128)}), f32[32,8,128]{2,1,0:T(8,128)S(1)}, u32[]{:S(2)}, u32[]{:S(2)}) async-start(f32[32,8,128]{2,1,0:T(8,128)} %add_shells.1), calls=%async_computation.6 | async-start | bytes 262144 | tf_op jit(solution)/shard_map/all_to_all | solution.py:442
  92.5 2.2 %bricks_back.1 = bf16[8,32,512]{2,1,0:T(8,128)(2,1)} custom-call(bf16[32,4096]{1,0:T(8,128)(2,1)S(1)} %get-tuple-element.48.cot, bf16[32,864]{1,0:T(8,128)(2,1)S(1)} %copy-done.2), custom_call_target="tpu_custom_call" | custom-call | flops 2000000000 | bytes 1000000 | tf_op jit(solution)/shard_map/bricks_back/pallas_call | solution.py:429
  94.8 5.6 %all-to-all-done.6.values = f32[32,8,128]{2,1,0:T(8,128)S(1)} async-done(((f32[32,8,128]{2,1,0:T(8,128)}), f32[32,8,128]{2,1,0:T(8,128)S(1)}, u32[]{:S(2)}, u32[]{:S(2)}) %all-to-all-start.6) | async-done | bytes 131104 | tf_op jit(solution)/shard_map/all_to_all | solution.py:442
  100.4 0.8 finish.1
  (1 shorter events, 0.0 us)
Async XLA Ops:
  0.6 10.2 %copy-start.2 = (bf16[32,864]{1,0:T(8,128)(2,1)S(1)}, bf16[32,864]{1,0:T(8,128)(2,1)}, u32[]{:S(2)}) copy-start(bf16[32,864]{1,0:T(8,128)(2,1)} %conv_w.3) | copy-start | bytes 165892
  2.1 8.8 %copy-start.4 = (bf16[32,64]{1,0:T(8,128)(2,1)S(1)}, bf16[32,64]{1,0:T(8,128)(2,1)}, u32[]{:S(2)}) copy-start(bf16[32,64]{1,0:T(8,128)(2,1)} %w1.3) | copy-start | bytes 12292
  2.1 16.0 %all-to-all-start = ((s32[32,1,256]{2,1,0:T(1,128)}), s32[32,1,256]{2,1,0:T(1,128)S(1)}, u32[]{:S(2)}, u32[]{:S(2)}) async-start(s32[32,1,256]{2,1,0:T(1,128)} %reshape_squeeze.3), calls=%async_computation | async-start | bytes 65536 | tf_op jit(solution)/shard_map/all_to_all | solution.py:442
  10.8 0.7 copy-start.10
  10.8 0.7 copy-start.8
  10.8 0.7 copy-start.9
  11.5 1.0 copy-start
  19.7 4.5 %copy-start.3 = (s32[1,4096]{1,0:T(1,128)S(1)}, s32[1,4096]{1,0:T(1,128)}, u32[]{:S(2)}) copy-start(s32[1,4096]{1,0:T(1,128)} %sources) | copy-start | bytes 49156
  19.7 4.5 %copy-start.6 = (f32[512]{0:T(512)S(1)}, f32[512]{0:T(512)}, u32[]{:S(2)}) copy-start(f32[512]{0:T(512)} %param.20) | copy-start | bytes 6148
  19.7 4.5 %copy-start.7 = (s32[512]{0:T(512)S(1)}, s32[512]{0:T(512)}, u32[]{:S(2)}) copy-start(s32[512]{0:T(512)} %param.21) | copy-start | bytes 6148
  19.7 11.8 %all-to-all-start.1 = ((f32[32,4,128]{2,1,0:T(4,128)}), f32[32,4,128]{2,1,0:T(4,128)S(1)}, u32[]{:S(2)}, u32[]{:S(2)}) async-start(f32[32,4,128]{2,1,0:T(4,128)} %owner_pick.1), calls=%async_computation.1 | async-start | bytes 131072 | tf_op jit(solution)/shard_map/all_to_all | solution.py:442
  24.2 0.7 copy-start.5
  47.7 13.6 %copy-start.1 = (bf16[1,8,32,512]{3,2,1,0:T(8,128)(2,1)S(1)}, bf16[1,8,32,512]{3,2,1,0:T(8,128)(2,1)}, u32[]{:S(2)}) copy-start(bf16[1,8,32,512]{3,2,1,0:T(8,128)(2,1)} %param.11) | copy-start | bytes 786436
  87.5 12.9 %all-to-all-start.6 = ((f32[32,8,128]{2,1,0:T(8,128)}), f32[32,8,128]{2,1,0:T(8,128)S(1)}, u32[]{:S(2)}, u32[]{:S(2)}) async-start(f32[32,8,128]{2,1,0:T(8,128)} %add_shells.1), calls=%async_computation.6 | async-start | bytes 262144 | tf_op jit(solution)/shard_map/all_to_all | solution.py:442

commit v5 on v4

--- a/solution.py
+++ b/solution.py
@@ -163,7 +163,8 @@
     return jnp.concatenate(parts, axis=1)
 
 
-def arrange_kernel(target, inten_target, drop, sources, targets_out, slots_out):
+def arrange_kernel(target, inten_target, drop, sources, bricks, targets_out, slots_out, columns_out):
+    columns_out[...] = c_columns(side_by_side(bricks, 0, bricks.shape[0]))
     targets_out[0:1, :] = target[...]
     targets_out[1:2, :] = inten_target[...]
     targets_out[2:3, :] = drop[...].astype(F32)
@@ -309,9 +310,9 @@
 
 
 def owner_back_kernel(
-    addr, cots, factor, dec, slope, bricks, w1, b1, w2t, loss, payload_out, cot_out, plane_s, ge_s
+    addr, cots, factor, dec, slope, columns, w1, b1, w2t, loss, payload_out, cot_out, plane_s, ge_s
 ):
-    count, ch = bricks.shape[0], bricks.shape[1]
+    count, ch = dec.shape[1] // CELLS, dec.shape[0]
     hid = w1.shape[1]
     groups = factor.shape[1]
     sectors = addr.shape[0]
@@ -356,7 +357,7 @@
         cot_out[:, cells] = cot
         wide = cot.astype(F32)
         acc_cb = acc_cb + fold_lanes(wide)
-        acc_cw = acc_cw + dot(ab_columns(wide), c_columns(side_by_side(bricks, first, M_BACK)), NT)
+        acc_cw = acc_cw + dot(ab_columns(wide), columns[:, cells], NT)
     lane = iota((ch, LANE), 1)
     tiles = [jnp.zeros((ch, LANE), F32) for _ in range(7)]
     pad = jnp.zeros((ch, LANE - 3 * ch), F32)
@@ -477,15 +478,16 @@
         flops=10**9,
         moved_bytes=10**5,
     )
-    targets, slots = call(
+    targets, slots, columns = call(
         arrange_kernel,
-        [((3, rays), F32), ((SAMP, rays), jnp.int32)],
-        [VMEM] * 4,
+        [((3, rays), F32), ((SAMP, rays), jnp.int32), ((3 * ch, cells), BF16)],
+        [VMEM] * 5,
         (
             depth_target.reshape(1, rays),
             inten_target.reshape(1, rays),
             drop_label.reshape(1, rays),
             lax.optimization_barrier((sample_src, picked))[0],
+            blocks,
         ),
         name="arrange",
         flops=10**9,
@@ -516,7 +518,7 @@
         owner_back_kernel,
         [((ch, 8, LANE), F32), ((ch, cells), BF16)],
         [VMEM] * 10,
-        (addr, cots, factor, dec, slope, blocks, head_w1, b1, w2t, loss),
+        (addr, cots, factor, dec, slope, columns, head_w1, b1, w2t, loss),
         scratch=[pltpu.VMEM((6, sectors, HI), F32), pltpu.VMEM((2, groups, HI), F32)],
         name="owner_back",
         flops=2 * 10**9,

time: 102 us -> 102 us (level)
  no operation moved by 1% of the time
where the time goes in v5:
time: 102 us; the launch traced here: 101 us
  blocking collectives  48 us (47%)
  starting transfers between devices  18.2 us (18%)
  Pallas kernels  15.3 us (15%)
  waiting for transfers between devices  15 us (15%)
  local copies, waits for them, and re-layouts  3.68 us (4%)
    all_to_all x4, blocking collectives, swap(): return lax.all_to_all(value, axis, split_axis=0, concat_axis=0, tiled=True)  48 us
    all_to_all x3, starting transfers between devices, swap(): return lax.all_to_all(value, axis, split_axis=0, concat_axis=0, tiled=True)  18.2 us
    pallas_call x10, Pallas kernels, call(): pl.pallas_call(kernel, out_shape=shapes, in_specs=specs, out_specs=out_sp...  15.3 us
    all_to_all x3, waiting for transfers between devices, swap(): return lax.all_to_all(value, axis, split_axis=0, concat_axis=0, tiled=True)  15 us
    unnamed x22, local copies, waits for them, and re-layouts  2.27 us
  transfers between devices with their start and end apart: 3, of which 3 were waited for; matrix products, arithmetic and copies ran while one was open for 0% of the time, Pallas kernels for 5%

profile of v5, /device:TPU:1, one launch (start us, length us, event | category | flops | bytes accessed | tf_op | source)
XLA Modules:
  0.0 101.0 jit_solution(9236564186173200590)
XLA Ops:
  0.6 0.0 copy-start.2
  0.6 1.4 %reshape_squeeze.3 = s32[32,1,256]{2,1,0:T(1,128)} reshape(s32[1,32,256]{2,1,0:T(8,128)} %param.17) | data formatting | bytes 65536 | tf_op jit(solution)/shard_map/reshape;squeeze | solution.py:461
  2.1 0.0 copy-start.4
  2.1 8.7 %all-to-all-start = ((s32[32,1,256]{2,1,0:T(1,128)}), s32[32,1,256]{2,1,0:T(1,128)S(1)}, u32[]{:S(2)}, u32[]{:S(2)}) async-start(s32[32,1,256]{2,1,0:T(1,128)} %reshape_squeeze.3), calls=%async_computation | async-start | bytes 65536 | tf_op jit(solution)/shard_map/all_to_all | solution.py:443
  10.8 0.0 copy-start.10
  10.8 0.0 copy-start.8
  10.8 0.0 copy-start.9
  10.8 0.0 copy-done.2
  10.8 0.0 copy-done.4
  10.8 0.6 copy-done.10
  11.4 0.0 copy-done.8
  11.5 0.0 copy-done.9
  11.5 0.0 copy-start
  11.5 0.9 copy-done
  12.4 2.6 %decode.1 = (bf16[32,4096]{1,0:T(8,128)(2,1)S(1)}, f32[32,4096]{1,0:T(8,128)S(1)}, bf16[96,256]{1,0:T(8,128)(2,1)S(1)}, f32[2,16,256]{2,1,0:T(8,128)S(1)}) custom-call(bf16[8,32,512]{2,1,0:T(8,128)(2,1)S(1)} %bitcast.14, bf16[32,864]{1,0:T(8,128)(2,1)S(1)} %copy-done.2, f32[1,32]{1,0:T(1,128)S(1)} %bitcast.21, bf16[32,64]{1,0:T(8,128)(2,1)S(1)} %copy-done.4, ...), custom_call_target="tpu_custom_call" | custom-call | flops 2000000000 | bytes 2000000 | tf_op jit(solution)/shard_map/decode/pallas_call | solution.py:430
  15.0 3.0 %all-to-all-done.addr = s32[32,1,256]{2,1,0:T(1,128)S(1)} async-done(((s32[32,1,256]{2,1,0:T(1,128)}), s32[32,1,256]{2,1,0:T(1,128)S(1)}, u32[]{:S(2)}, u32[]{:S(2)}) %all-to-all-start) | async-done | bytes 32800 | tf_op jit(solution)/shard_map/all_to_all | solution.py:443
  18.1 0.0 copy-start.1
  18.1 1.6 %owner_pick.1 = f32[32,4,128]{2,1,0:T(4,128)} custom-call(s32[32,1,256]{2,1,0:T(1,128)S(1)} %all-to-all-done.addr, bf16[96,256]{1,0:T(8,128)(2,1)S(1)} %get-tuple-element.30.planes), custom_call_target="tpu_custom_call" | custom-call | flops 1000000000 | bytes 100000 | tf_op jit(solution)/shard_map/owner_pick/pallas_call | solution.py:430
  19.7 0.0 copy-start.3
  19.7 0.0 copy-start.6
  19.7 0.0 copy-start.7
  19.7 4.5 %all-to-all-start.1 = ((f32[32,4,128]{2,1,0:T(4,128)}), f32[32,4,128]{2,1,0:T(4,128)S(1)}, u32[]{:S(2)}, u32[]{:S(2)}) async-start(f32[32,4,128]{2,1,0:T(4,128)} %owner_pick.1), calls=%async_computation.1 | async-start | bytes 131072 | tf_op jit(solution)/shard_map/all_to_all | solution.py:443
  24.2 0.0 copy-start.5
  24.2 0.0 copy-done.1
  24.2 0.0 copy-done.3
  24.2 0.0 copy-done.6
  24.2 0.0 copy-done.7
  24.2 0.6 copy-done.5
  24.8 0.3 arrange.1
  25.1 6.4 %all-to-all-done.1.replies = f32[32,4,128]{2,1,0:T(4,128)S(1)} async-done(((f32[32,4,128]{2,1,0:T(4,128)}), f32[32,4,128]{2,1,0:T(4,128)S(1)}, u32[]{:S(2)}, u32[]{:S(2)}) %all-to-all-start.1) | async-done | bytes 65568 | tf_op jit(solution)/shard_map/all_to_all | solution.py:443
  31.5 0.9 sample.1
  32.4 15.2 %all_to_all.35.terms = f32[8,4,512]{2,1,0:T(4,128)S(1)} all-to-all(f32[8,4,512]{2,1,0:T(4,128)S(1)} %get-tuple-element.33), channel_id=1, replica_groups=mesh['shell'=8,'sector'=32] {'shell'}, dimensions={0} | all-to-all | bytes 131072 | tf_op jit(solution)/shard_map/all_to_all | solution.py:443
  47.7 1.3 %render.1 = (f32[32,4,128]{2,1,0:T(4,128)S(1)}, f32[1,512]{1,0:T(1,128)}, f32[1,1]{1,0:T(1,128)}) custom-call(s32[1]{0:T(128)} %bitcast.shell_ref, f32[8,4,512]{2,1,0:T(4,128)S(1)} %all_to_all.35.terms, f32[8,512]{1,0:T(8,128)S(1)} %get-tuple-element.34.density, f32[8,512]{1,0:T(8,128)S(1)} %get-tuple-element.35.intensity, ...), custom_call_target="tpu_custom_call" | custom-call | flops 1000000000 | bytes 100000 | tf_op jit(solution)/shard_map/render/pallas_call | solution.py:430
  49.0 12.3 %all_to_all.36.cots = f32[32,4,128]{2,1,0:T(4,128)S(1)} all-to-all(f32[32,4,128]{2,1,0:T(4,128)S(1)} %get-tuple-element.37), channel_id=1, replica_groups=mesh['shell'=8,'sector'=32] {'sector'}, dimensions={0} | all-to-all | bytes 131072 | tf_op jit(solution)/shard_map/all_to_all | solution.py:443
  61.3 4.9 %owner_back.1 = (f32[32,8,128]{2,1,0:T(8,128)S(1)}, bf16[32,4096]{1,0:T(8,128)(2,1)S(1)}) custom-call(s32[32,1,256]{2,1,0:T(1,128)S(1)} %all-to-all-done.addr, f32[32,4,128]{2,1,0:T(4,128)S(1)} %all_to_all.36.cots, f32[2,16,256]{2,1,0:T(8,128)S(1)} %get-tuple-element.38.factor, bf16[32,4096]{1,0:T(8,128)(2,1)S(1)} %get-tuple-element.39.dec, ...), custom_call_target="tpu_custom_call" | custom-call | flops 2000000000 | bytes 2000000 | tf_op jit(solution)/shard_map/owner_back/pallas_call | solution.py:430
  66.2 11.2 %all_to_all.37.values = f32[32,8,128]{2,1,0:T(8,128)S(1)} all-to-all(f32[32,8,128]{2,1,0:T(8,128)S(1)} %get-tuple-element.43), channel_id=1, replica_groups=mesh['shell'=8,'sector'=32] {'sector'}, dimensions={0} | all-to-all | bytes 262144 | tf_op jit(solution)/shard_map/all_to_all | solution.py:443
  77.5 9.2 %all_to_all.38.values = f32[8,8,128]{2,1,0:T(8,128)S(1)} all-to-all(f32[8,8,128]{2,1,0:T(8,128)S(1)} %add_sectors.1), channel_id=1, replica_groups=mesh['shell'=8,'sector'=32] {'shell'}, dimensions={0} | all-to-all | bytes 65536 | tf_op jit(solution)/shard_map/all_to_all | solution.py:443
  86.7 0.7 add_shells.1
  87.4 5.0 %all-to-all-start.6 = ((f32[32,8,128]{2,1,0:T(8,128)}), f32[32,8,128]{2,1,0:T(8,128)S(1)}, u32[]{:S(2)}, u32[]{:S(2)}) async-start(f32[32,8,128]{2,1,0:T(8,128)} %add_shells.1), calls=%async_computation.6 | async-start | bytes 262144 | tf_op jit(solution)/shard_map/all_to_all | solution.py:443
  92.4 2.2 %bricks_back.1 = bf16[8,32,512]{2,1,0:T(8,128)(2,1)} custom-call(bf16[32,4096]{1,0:T(8,128)(2,1)S(1)} %get-tuple-element.50.cot, bf16[32,864]{1,0:T(8,128)(2,1)S(1)} %copy-done.2), custom_call_target="tpu_custom_call" | custom-call | flops 2000000000 | bytes 1000000 | tf_op jit(solution)/shard_map/bricks_back/pallas_call | solution.py:430
  94.6 5.6 %all-to-all-done.6.values = f32[32,8,128]{2,1,0:T(8,128)S(1)} async-done(((f32[32,8,128]{2,1,0:T(8,128)}), f32[32,8,128]{2,1,0:T(8,128)S(1)}, u32[]{:S(2)}, u32[]{:S(2)}) %all-to-all-start.6) | async-done | bytes 131104 | tf_op jit(solution)/shard_map/all_to_all | solution.py:443
  100.3 0.8 finish.1
  (1 shorter events, 0.0 us)
Async XLA Ops:
  0.6 10.2 %copy-start.2 = (bf16[32,864]{1,0:T(8,128)(2,1)S(1)}, bf16[32,864]{1,0:T(8,128)(2,1)}, u32[]{:S(2)}) copy-start(bf16[32,864]{1,0:T(8,128)(2,1)} %conv_w.3) | copy-start | bytes 165892
  2.1 8.8 %copy-start.4 = (bf16[32,64]{1,0:T(8,128)(2,1)S(1)}, bf16[32,64]{1,0:T(8,128)(2,1)}, u32[]{:S(2)}) copy-start(bf16[32,64]{1,0:T(8,128)(2,1)} %w1.3) | copy-start | bytes 12292
  2.1 16.0 %all-to-all-start = ((s32[32,1,256]{2,1,0:T(1,128)}), s32[32,1,256]{2,1,0:T(1,128)S(1)}, u32[]{:S(2)}, u32[]{:S(2)}) async-start(s32[32,1,256]{2,1,0:T(1,128)} %reshape_squeeze.3), calls=%async_computation | async-start | bytes 65536 | tf_op jit(solution)/shard_map/all_to_all | solution.py:443
  10.8 0.7 copy-start.10
  10.8 0.7 copy-start.8
  10.8 0.7 copy-start.9
  11.5 1.0 copy-start
  18.1 6.1 %copy-start.1 = (bf16[1,8,32,512]{3,2,1,0:T(8,128)(2,1)S(1)}, bf16[1,8,32,512]{3,2,1,0:T(8,128)(2,1)}, u32[]{:S(2)}) copy-start(bf16[1,8,32,512]{3,2,1,0:T(8,128)(2,1)} %param.11) | copy-start | bytes 786436
  19.7 4.5 %copy-start.3 = (s32[1,4096]{1,0:T(1,128)S(1)}, s32[1,4096]{1,0:T(1,128)}, u32[]{:S(2)}) copy-start(s32[1,4096]{1,0:T(1,128)} %sources) | copy-start | bytes 49156
  19.7 4.5 %copy-start.6 = (f32[512]{0:T(512)S(1)}, f32[512]{0:T(512)}, u32[]{:S(2)}) copy-start(f32[512]{0:T(512)} %param.20) | copy-start | bytes 6148
  19.7 4.5 %copy-start.7 = (s32[512]{0:T(512)S(1)}, s32[512]{0:T(512)}, u32[]{:S(2)}) copy-start(s32[512]{0:T(512)} %param.21) | copy-start | bytes 6148
  19.7 11.9 %all-to-all-start.1 = ((f32[32,4,128]{2,1,0:T(4,128)}), f32[32,4,128]{2,1,0:T(4,128)S(1)}, u32[]{:S(2)}, u32[]{:S(2)}) async-start(f32[32,4,128]{2,1,0:T(4,128)} %owner_pick.1), calls=%async_computation.1 | async-start | bytes 131072 | tf_op jit(solution)/shard_map/all_to_all | solution.py:443
  24.2 0.7 copy-start.5
  87.4 12.9 %all-to-all-start.6 = ((f32[32,8,128]{2,1,0:T(8,128)}), f32[32,8,128]{2,1,0:T(8,128)S(1)}, u32[]{:S(2)}, u32[]{:S(2)}) async-start(f32[32,8,128]{2,1,0:T(8,128)} %add_shells.1), calls=%async_computation.6 | async-start | bytes 262144 | tf_op jit(solution)/shard_map/all_to_all | solution.py:443
